TPU v7x, 32 devices: a whole 2x2x4 slice. The times are simulated.
32 devices in a mesh: groups: 2 (over y), replica: 1, da: 4 (over x, core), db: 4 (over z).
Axes of the slice: x: 2, y: 2, z: 4, core: 2. Of those that a mesh axis runs over, the one named last changes fastest.
Arguments:
- tokens: bfloat16 [4096, 1024], P(('groups', 'replica', 'da', 'db')), parts along dimension 0, may hold values from -6 to 6
- grad_out: bfloat16 [4096, 1024], P(('groups', 'replica', 'da', 'db')), parts along dimension 0, may hold values from -3 to 3
- routes: int32 [4096, 8], P(('groups', 'replica', 'da', 'db')), parts along dimension 0, may hold values from 0 to 15, as said below
- gates: bfloat16 [4096, 8], P(('groups', 'replica', 'da', 'db')), parts along dimension 0, may hold values from 0.019897461 to 0.5
- w_gate_up: bfloat16 [16, 1024, 768], P(('da', 'db'), 'replica'), may hold values from -0.1875 to 0.1875
- w_down: bfloat16 [16, 384, 1024], P(('da', 'db'), 'replica'), may hold values from -0.3125 to 0.3125
Outputs:
- token_grads: bfloat16 [4096, 1024], P(('groups', 'replica', 'da', 'db')), parts along dimension 0
- gate_grads: bfloat16 [4096, 8], P(('groups', 'replica', 'da', 'db')), parts along dimension 0
- gate_up_grads: bfloat16 [32, 1024, 768], P(('groups', 'da', 'db'), 'replica'), parts along dimension 0
- down_grads: bfloat16 [32, 384, 1024], P(('groups', 'da', 'db'), 'replica'), parts along dimension 0
There are 2 independent parts, one for each index of `groups`. A program takes and returns all parts, laid end to end along the dimension named above; an argument that names none is the same for every part. Nothing has to cross between parts.
Inputs may be any that keep to these rules, and one draw needn't show every extreme that they name: `routes`: each token names 8 different experts. In every aligned block of 2 consecutive tokens, each expert is named exactly once, so the tokens of one device name every expert exactly 64 times.
All inputs are finite; a program needn't handle non-finite values.
Results may differ from a plain program's by a relative error of at most 0.0085.
Values may be sent and summed in bfloat16 or wider, within the bound.
A program may use at most 64 MiB of HBM per device.

v0:
```python
import functools

import jax
import jax.numpy as jnp
from jax import lax
from jax.experimental import pallas as pl
from jax.experimental.pallas import tpu as pltpu
from jax.sharding import PartitionSpec as P


CORES = 2
PIECES = 4
MESH = pl.DeviceIdType.MESH


def silu_parts(projected):
    sigmoid = jax.nn.sigmoid(projected)
    return (projected * sigmoid, sigmoid * (1.0 + projected * (1.0 - sigmoid)))


def body(tokens, grad_out, routes, gates, w_gate_up, w_down):
    local_tokens, features = tokens.shape
    top_count = routes.shape[1]
    hidden_units = w_gate_up.shape[2] // 2
    first_size = lax.axis_size("da")
    second_size = lax.axis_size("db")
    experts = first_size * second_size
    per_round = experts // top_count
    rounds = local_tokens // per_round
    expert_ids = lax.broadcasted_iota(jnp.int32, (1, 1, 1, experts), 3)
    matches = routes.reshape(rounds, per_round, top_count, 1) == expert_ids
    gate_values = gates.reshape(rounds, per_round, top_count, 1).astype(jnp.float32)
    gate_table = jnp.sum(jnp.where(matches, gate_values, 0.0), axis=(1, 2)).astype(jnp.bfloat16)
    chosen = jnp.any(matches, axis=2).astype(jnp.bfloat16)
    input_send = jnp.einsum(
        "rge,rgd->red",
        chosen,
        tokens.reshape(rounds, per_round, features),
        preferred_element_type=jnp.float32,
    ).astype(jnp.bfloat16)
    upstream_send = jnp.einsum(
        "rge,rgd->red",
        chosen,
        grad_out.reshape(rounds, per_round, features),
        preferred_element_type=jnp.float32,
    ).astype(jnp.bfloat16)
    input_recv, upstream_recv, gate_recv = (
        lax.all_to_all(input_send, ("da", "db"), split_axis=1, concat_axis=1, tiled=True),
        lax.all_to_all(upstream_send, ("da", "db"), split_axis=1, concat_axis=1, tiled=True),
        lax.all_to_all(gate_table, ("da", "db"), split_axis=1, concat_axis=1, tiled=True),
    )
    input_rows = input_recv.reshape(-1, features)
    upstream_rows = upstream_recv.reshape(-1, features)
    gate_rows = gate_recv.reshape(-1, 1).astype(jnp.float32)
    w_in, w_out = (
        lax.all_gather(w_gate_up[0], "replica", axis=0, tiled=True),
        lax.all_gather(w_down[0], "replica", axis=0, tiled=True),
    )
    projected = jnp.dot(input_rows, w_in, preferred_element_type=jnp.float32)
    back_raw = jnp.einsum("rd,fd->rf", upstream_rows, w_out, preferred_element_type=jnp.float32)
    gate_part = projected[:, :hidden_units]
    up_part = projected[:, hidden_units:]
    activated, derivative = silu_parts(gate_part)
    hidden = (activated * up_part).astype(jnp.bfloat16)
    gate_scores = jnp.sum(hidden.astype(jnp.float32) * back_raw, axis=1).astype(jnp.bfloat16)
    back_hidden = gate_rows * back_raw
    grad_projected = jnp.concatenate(
        [back_hidden * up_part * derivative, back_hidden * activated], axis=1
    ).astype(jnp.bfloat16)
    scaled_upstream = (gate_rows * upstream_rows.astype(jnp.float32)).astype(jnp.bfloat16)
    input_grads = jnp.einsum("rf,df->rd", grad_projected, w_in, preferred_element_type=jnp.float32)
    input_grads = input_grads.astype(jnp.bfloat16).reshape(rounds, experts, features)
    score_back = gate_scores.reshape(rounds, experts)
    returned, score_ret = (
        lax.all_to_all(input_grads, ("da", "db"), split_axis=1, concat_axis=1, tiled=True),
        lax.all_to_all(score_back, ("da", "db"), split_axis=1, concat_axis=1, tiled=True),
    )
    score_ret = score_ret.reshape(rounds, 1, 1, experts).astype(jnp.float32)
    token_grads = (
        jnp.einsum("rge,red->rgd", chosen, returned, preferred_element_type=jnp.float32)
        .astype(jnp.bfloat16)
        .reshape(local_tokens, features)
    )
    gate_grads = (
        jnp.sum(jnp.where(matches, score_ret, 0.0), axis=3)
        .astype(jnp.bfloat16)
        .reshape(local_tokens, top_count)
    )
    columns = input_rows
    grad_in = lax.psum_scatter(
        jnp.einsum("rd,rf->df", columns, grad_projected, preferred_element_type=jnp.float32).astype(
            jnp.bfloat16
        ),
        "replica",
        scatter_dimension=0,
        tiled=True,
    )
    columns = hidden
    grad_down = lax.psum_scatter(
        jnp.einsum(
            "rf,rd->fd", columns, scaled_upstream, preferred_element_type=jnp.float32
        ).astype(jnp.bfloat16),
        "replica",
        scatter_dimension=0,
        tiled=True,
    )
    return (token_grads, gate_grads, grad_in[None], grad_down[None])


def visit(j, z, n):
    m = jnp.minimum(z, n - 1 - z)
    near = z + (1 - 2 * (j % 2)) * ((j + 1) // 2)
    far = jnp.where(z < n - 1 - z, j, n - 1 - j)
    return jnp.where(j <= 2 * m, near, far)


def dot(a, b, dims):
    return lax.dot_general(a, b, (dims, ((), ())), preferred_element_type=jnp.float32)


def fused_kernel(
    cols, depth, group,
    tok_hbm, up_hbm, routes_hbm, gates_hbm, win_hbm, wout_hbm,
    tg_ref, gg_ref, gin_ref, gdown_ref,
    routes_ref, gates_ref, tok, up, table, win, wout, xs, su, hid, gp, igs, igb, ps, pk, pr, rs, rk, rz, scs, scr,
    load_sem, recv_sem, zup_sem, zdn_sem, x_sem, o_sem, p_sem, igs_sem, igr_sem, ps_sem, pr_sem, rs_sem, rz_sem,
    scs_sem, scr_sem,
):
    da = lax.axis_index("da")
    z = lax.axis_index("db")
    x, c = da // CORES, da % CORES
    local, features = tok.shape[1], tok.shape[2]
    experts = table.shape[1]
    top = routes_ref.shape[0]
    rows = local // group
    ff = wout.shape[0]
    others = cols - 1

    def slot(xx, zz, cc):
        return (xx * CORES + cc) * depth + zz

    me = slot(x, z, c)
    loads = [
        pltpu.make_async_copy(tok_hbm, tok.at[me], load_sem.at[0]),
        pltpu.make_async_copy(up_hbm, up.at[me], load_sem.at[1]),
        pltpu.make_async_copy(win_hbm.at[0], win, load_sem.at[2]),
        pltpu.make_async_copy(wout_hbm.at[0], wout, load_sem.at[3]),
        pltpu.make_async_copy(routes_hbm, routes_ref, load_sem.at[4]),
        pltpu.make_async_copy(gates_hbm, gates_ref, load_sem.at[5]),
    ]
    for k in (4, 5, 0, 1, 2, 3):
        loads[k].start()

    barrier = pltpu.get_barrier_semaphore()
    count = cols * CORES * depth

    @pl.loop(1, count)
    def _(k):
        to = (me + k) % count
        pl.semaphore_signal(
            barrier, inc=1, device_id={"da": to // depth, "db": to % depth}, device_id_type=MESH
        )

    loads[4].wait()
    loads[5].wait()
    routes = routes_ref[...]
    gates = gates_ref[...].astype(jnp.float32)
    ids = lax.broadcasted_iota(jnp.int32, (experts, local), 0)
    chart = jnp.zeros((experts, local), jnp.float32)
    for k in range(top):
        chart = chart + jnp.where(routes[k : k + 1] == ids, gates[k : k + 1], 0.0)
    table[me] = chart.astype(jnp.bfloat16)

    pl.semaphore_wait(barrier, count - 1)
    loads[0].wait()
    loads[1].wait()

    held = (table, tok, up)

    def send(src, dst, send_sem, recv, to_x, to_z, to_c):
        return pltpu.make_async_remote_copy(
            src_ref=src,
            dst_ref=dst,
            send_sem=send_sem,
            recv_sem=recv,
            device_id={"da": to_x * CORES + to_c, "db": to_z},
            device_id_type=MESH,
        )

    def relay(s, a, sem, to_x, to_z, to_c):
        ref = held[a].at[s]
        return send(ref, ref, sem, recv_sem.at[s, a], to_x, to_z, to_c)

    def arrive(s):
        for a in range(3):
            relay(s, a, p_sem.at[0, 0, a], x, z, 1 - c).wait_recv()

    def along(row, zz, a):
        last = depth - 1
        near = ((row == 1) & (zz == 0)) | ((row == last - 1) & (zz == last))
        if a != 2:
            return near
        return near | ((row == 0) & (zz == last)) | ((row == last) & (zz == 0))

    def spread_column(zz, act, await_first=None):
        s = slot(x, zz, c)
        for a in range(3):
            if await_first is not None:

                @pl.when(await_first)
                def _():
                    relay(s, a, p_sem.at[0, 0, a], x, z, 1 - c).wait_recv()

            @pl.when((zz <= z) & (z < depth - 1))
            def _():
                act(relay(s, a, zup_sem.at[zz, a], x, z + 1, c))

            @pl.when((zz >= z) & (z > 0))
            def _():
                act(relay(s, a, zdn_sem.at[zz, a], x, z - 1, c))

            for o in range(others):

                @pl.when(jnp.logical_not(along(z, zz, a)))
                def _():
                    act(relay(s, a, x_sem.at[o, zz, a], (x + 1 + o) % cols, z, c))

            act(relay(s, a, p_sem.at[0, zz, a], x, z, 1 - c))

    def spread_core(o, zz, act):
        s = slot((x + 1 + o) % cols, zz, c)
        last = depth - 1
        for a in range(3):
            up = ((z == 0) & along(1, zz, a)) | ((z == last - 1) & along(last, zz, a) & (zz == 0))
            down = ((z == last) & along(last - 1, zz, a)) | ((z == 1) & along(0, zz, a) & (zz == last))
            up = up & jnp.logical_not((z == 0) & (zz != 0))
            down = down & jnp.logical_not((z == last) & (zz != last))

            @pl.when(up)
            def _():
                act(relay(s, a, o_sem.at[o, zz, a], x, z + 1, c))

            @pl.when(down)
            def _():
                act(relay(s, a, o_sem.at[o, zz, a], x, z - 1, c))

        for a in range(3):
            act(relay(s, a, p_sem.at[1 + o, zz, a], x, z, 1 - c))

    def pick(s, e):
        chart_s = table[s].astype(jnp.float32)
        which = lax.broadcasted_iota(jnp.int32, chart_s.shape, 0) == e
        row = jnp.sum(jnp.where(which, chart_s, 0.0), axis=0, keepdims=True)
        off = lax.broadcasted_iota(jnp.int32, (rows, local), 1) - group * lax.broadcasted_iota(
            jnp.int32, (rows, local), 0
        )
        hit = (off >= 0) & (off < group) & (row > 0.0)
        return jnp.where(hit, 1.0, 0.0), row

    def send_ig(i, zz):
        xx = (x + i) % cols
        return send(
            igs.at[xx, zz], igb.at[xx, zz, c], igs_sem.at[xx, zz], igr_sem.at[xx, zz], x, z, 1 - c
        )

    def send_score(s):
        return pltpu.make_async_remote_copy(
            src_ref=scs.at[s],
            dst_ref=scr.at[me],
            send_sem=scs_sem.at[s],
            recv_sem=scr_sem.at[me],
            device_id={"da": s // depth, "db": s % depth},
            device_id_type=MESH,
        )

    span = local // PIECES

    def part(h):
        return pl.ds(h * span, span)

    def send_part(o, zz, h):
        return send(
            ps.at[o, zz, part(h)],
            pr.at[others - 1 - o, zz, part(h)],
            ps_sem.at[o, zz, h],
            pr_sem.at[others - 1 - o, zz, h],
            (x + 1 + o) % cols,
            z,
            c,
        )

    def send_row(zz, h):
        return send(rs.at[zz, part(h)], rz.at[z, part(h)], rs_sem.at[zz, h], rz_sem.at[z, h], x, zz, c)

    blocks = [(i, r) for i in range(cols) for r in range(CORES)]
    batch = len(blocks) * rows

    def compute(j, zz):
        base = pl.multiple_of(j * batch, batch)
        picks = []
        gate_cols = []
        for n, (i, r) in enumerate(blocks):
            s = slot((x + i) % cols, zz, (c + r) % CORES)
            chosen, row = pick(s, me)
            picks.append((s, chosen))
            gate_cols.append(jnp.sum(chosen * row, axis=1, keepdims=True))
            hot = chosen.astype(jnp.bfloat16)
            where = pl.ds(pl.multiple_of(base + n * rows, rows), rows)
            xs[where, :] = dot(hot, tok[s], ((1,), (0,))).astype(jnp.bfloat16)
            su[where, :] = dot(hot, up[s], ((1,), (0,))).astype(jnp.bfloat16)
        here = pl.ds(base, batch)
        gate = jnp.concatenate(gate_cols, axis=0)
        upstream = su[here, :]
        projected = dot(xs[here, :], win[...], ((1,), (0,)))
        back_raw = dot(upstream, wout[...], ((1,), (1,)))
        su[here, :] = (gate * upstream.astype(jnp.float32)).astype(jnp.bfloat16)
        gate_part, up_part = projected[:, :ff], projected[:, ff:]
        activated, derivative = silu_parts(gate_part)
        hidden = (activated * up_part).astype(jnp.bfloat16)
        hid[here, :] = hidden
        scores = jnp.sum(hidden.astype(jnp.float32) * back_raw, axis=1, keepdims=True)
        scores = scores.astype(jnp.bfloat16).astype(jnp.float32)
        back_hidden = gate * back_raw
        gp[here, :ff] = (back_hidden * up_part * derivative).astype(jnp.bfloat16)
        gp[here, ff:] = (back_hidden * activated).astype(jnp.bfloat16)
        grads = dot(gp[here, :], win[...], ((1,), (1,))).astype(jnp.bfloat16)
        for n, (i, r) in enumerate(blocks):
            xx = (x + i) % cols
            piece = grads[n * rows : (n + 1) * rows]
            if r == 0:
                igb[xx, zz, c] = piece
            else:
                igs[xx, zz] = piece
                send_ig(i, zz).start()
        for n, (i, r) in enumerate(blocks):
            s, chosen = picks[n]
            line = jnp.sum(chosen * scores[n * rows : (n + 1) * rows], axis=0, keepdims=True)
            scs[s] = jnp.broadcast_to(line, scs.shape[1:])
            if i == 0 and r == 0:

                @pl.when(zz == z)
                def _():
                    scr[me] = scs[me]

                @pl.when(zz != z)
                def _():
                    send_score(s).start()
            else:
                send_score(s).start()

    def chip_sum(i, zz):
        xx = (x + i) % cols
        s = slot(xx, zz, c)
        hot = jnp.concatenate([pick(s, slot(x, z, k))[0] for k in range(CORES)], axis=0)
        both = igb[xx, zz].reshape(CORES * rows, features)
        return dot(hot.astype(jnp.bfloat16), both, ((0,), (0,)))

    def start(copy):
        copy.start()

    def wait_send(copy):
        copy.wait_send()

    def step(i, carry):
        @pl.when(i < depth)
        def _():
            zz = visit(i, z, depth)

            spread_column(zz, start, i > 0)

        @pl.when((i >= 2) & (i < depth + 2))
        def _():
            j = i - 2
            zz = visit(j, z, depth)

            @pl.when(j == 0)
            def _():
                loads[2].wait()
                loads[3].wait()

            for k in range(cols):
                arrive(slot((x + k) % cols, zz, 1 - c))
            compute(j, zz)
            for k in list(range(1, cols)) + [0]:
                send_ig(k, zz).wait_recv()
                total = chip_sum(k, zz)
                if k == 0:
                    pk[zz] = total
                else:
                    ps[k - 1, zz] = total.astype(jnp.bfloat16)
                    for h in range(PIECES):
                        send_part(k - 1, zz, h).start()

        @pl.when((i >= 1) & (i <= depth))
        def _():
            zz = visit(i - 1, z, depth)
            for o in range(others):
                arrive(slot((x + 1 + o) % cols, zz, c))
                spread_core(o, zz, start)

        @pl.when(i >= 4)
        def _():
            zz = visit(i - 4, z, depth)
            for h in range(PIECES):
                total = pk[zz, part(h)]
                for o in range(others):
                    send_part(others - 1 - o, zz, h).wait_recv()
                    total = total + pr[o, zz, part(h)].astype(jnp.float32)

                @pl.when(zz == z)
                def _():
                    rk[part(h), :] = total

                @pl.when(zz != z)
                def _():
                    rs[zz, part(h)] = total.astype(jnp.bfloat16)
                    send_row(zz, h).start()

        return carry

    lax.fori_loop(0, depth + 4, step, 0)

    wide = min(features, 256)

    @pl.loop(0, features // wide)
    def _(t):
        at = pl.ds(pl.multiple_of(t * wide, wide), wide)
        gin_ref[0, at, :] = dot(xs[:, at], gp[...], ((0,), (0,))).astype(jnp.bfloat16)

    thin = 128

    @pl.loop(0, ff // thin)
    def _(t):
        at = pl.ds(pl.multiple_of(t * thin, thin), thin)
        gdown_ref[0, at, :] = dot(hid[:, at], su[...], ((0,), (0,))).astype(jnp.bfloat16)

    @pl.loop(1, count)
    def _(k):
        s = (me + k) % count
        pltpu.make_async_remote_copy(
            src_ref=scs.at[s],
            dst_ref=scr.at[s],
            send_sem=scs_sem.at[s],
            recv_sem=scr_sem.at[s],
            device_id={"da": s // depth, "db": s % depth},
            device_id_type=MESH,
        ).wait()

    scores = scr[:, 0, :]
    place = lax.broadcasted_iota(jnp.int32, (top, local), 0)
    gate_grads = jnp.zeros((top, local), jnp.float32)
    for k in range(top):
        value = jnp.sum(jnp.where(routes[k : k + 1] == ids, scores, 0.0), axis=0, keepdims=True)
        gate_grads = jnp.where(place == k, value, gate_grads)
    gg_ref[...] = gate_grads.astype(jnp.bfloat16)

    def finish(k, carry):
        zz = (z + k) % depth
        for h in range(PIECES):
            send(
                rs.at[zz, part(h)], rz.at[zz, part(h)], rs_sem.at[zz, h], rz_sem.at[zz, h], x, zz, c
            ).wait()
            rk[part(h), :] += rz[zz, part(h)].astype(jnp.float32)
        return carry

    lax.fori_loop(1, depth, finish, 0)
    tg_ref[...] = rk[...].astype(jnp.bfloat16)

    def drain(zz, carry):
        spread_column(zz, wait_send)
        for o in range(others):
            spread_core(o, zz, wait_send)
            for h in range(PIECES):
                send_part(o, zz, h).wait_send()
        for k in range(cols):
            send_ig(k, zz).wait_send()
        return carry

    lax.fori_loop(0, depth, drain, 0)


def store_kernel(*refs):
    count = len(refs) // 2
    sems = refs[-1]
    copies = [
        pltpu.make_async_copy(refs[k], refs[count + k], sems.at[k]) for k in range(count)
    ]
    for one in copies:
        one.start()
    for one in copies:
        one.wait()


def store(*arrays):
    anywhere = pl.BlockSpec(memory_space=pl.ANY)
    return pl.pallas_call(
        store_kernel,
        out_shape=tuple(jax.ShapeDtypeStruct(a.shape, a.dtype) for a in arrays),
        in_specs=[pl.BlockSpec(memory_space=pltpu.VMEM)] * len(arrays),
        out_specs=(pl.BlockSpec(memory_space=pltpu.HBM),) * len(arrays),
        scratch_shapes=[pltpu.SemaphoreType.DMA((len(arrays),))],
        compiler_params=pltpu.CompilerParams(vmem_limit_bytes=8 * 2**20),
    )(*arrays)


def fused(tokens, grad_out, routes, gates, w_gate_up, w_down):
    first_size, depth = lax.axis_size("da"), lax.axis_size("db")
    cols = first_size // CORES
    experts = first_size * depth
    local, features = tokens.shape
    top = routes.shape[1]
    group = experts // top
    rows = local // group
    ff = w_down.shape[1]
    bf, f32 = jnp.bfloat16, jnp.float32
    total = rows * experts
    dma = pltpu.SemaphoreType.DMA
    scratch = [
        pltpu.VMEM((top, local), routes.dtype),
        pltpu.VMEM((top, local), gates.dtype),
        pltpu.VMEM((experts, local, features), bf),
        pltpu.VMEM((experts, local, features), bf),
        pltpu.VMEM((experts, experts, local), bf),
        pltpu.VMEM((features, 2 * ff), bf),
        pltpu.VMEM((ff, features), bf),
        pltpu.VMEM((total, features), bf),
        pltpu.VMEM((total, features), bf),
        pltpu.VMEM((total, ff), bf),
        pltpu.VMEM((total, 2 * ff), bf),
        pltpu.VMEM((cols, depth, rows, features), bf),
        pltpu.VMEM((cols, depth, CORES, rows, features), bf),
        pltpu.VMEM((cols - 1, depth, local, features), bf),
        pltpu.VMEM((depth, local, features), f32),
        pltpu.VMEM((cols - 1, depth, local, features), bf),
        pltpu.VMEM((depth, local, features), bf),
        pltpu.VMEM((local, features), f32),
        pltpu.VMEM((depth, local, features), bf),
        pltpu.VMEM((experts, 8, local), f32),
        pltpu.VMEM((experts, 8, local), f32),
        dma((6,)),
        dma((experts, 3)),
        dma((depth, 3)),
        dma((depth, 3)),
        dma((cols - 1, depth, 3)),
        dma((cols - 1, depth, 3)),
        dma((cols, depth, 3)),
        dma((cols, depth)),
        dma((cols, depth)),
        dma((cols - 1, depth, PIECES)),
        dma((cols - 1, depth, PIECES)),
        dma((depth, PIECES)),
        dma((depth, PIECES)),
        dma((experts,)),
        dma((experts,)),
    ]
    vmem = pl.BlockSpec(memory_space=pltpu.VMEM)
    hbm = pl.BlockSpec(memory_space=pltpu.HBM)
    token_grads, gate_grads, grad_in, grad_down = pl.pallas_call(
        functools.partial(fused_kernel, cols, depth, group),
        out_shape=(
            jax.ShapeDtypeStruct((local, features), bf),
            jax.ShapeDtypeStruct((top, local), bf),
            jax.ShapeDtypeStruct(w_gate_up.shape, bf),
            jax.ShapeDtypeStruct(w_down.shape, bf),
        ),
        in_specs=[hbm] * 6,
        out_specs=(vmem, vmem, vmem, vmem),
        scratch_shapes=scratch,
        compiler_params=pltpu.CompilerParams(
            collective_id=0, has_side_effects=True, vmem_limit_bytes=44 * 2**20
        ),
    )(
        *(
            pltpu.with_memory_space_constraint(a, pltpu.HBM)
            for a in (tokens, grad_out, routes.T, gates.T, w_gate_up, w_down)
        )
    )
    token_grads, gate_grads, grad_in, grad_down = store(token_grads, gate_grads, grad_in, grad_down)
    return token_grads, gate_grads.T, grad_in, grad_down


def fits(tokens, routes, w_down):
    first_size = lax.axis_size("da")
    experts = first_size * lax.axis_size("db")
    local, features = tokens.shape
    group = experts // routes.shape[1]
    held = 2 * experts * local * features * 2
    return (
        lax.axis_size("replica") == 1
        and first_size % CORES == 0
        and first_size > CORES
        and lax.axis_size("db") >= 4
        and held <= 16 * 2**20
        and local == 128
        and experts <= local
        and (local // group) % 16 == 0
        and w_down.shape[1] % 128 == 0
    )


def route(*arrays):
    if fits(arrays[0], arrays[2], arrays[5]):
        return fused(*arrays)
    return body(*arrays)


def solution(mesh):
    placed = (
        P(("groups", "replica", "da", "db"), None),
        P(("groups", "replica", "da", "db"), None),
        P(("groups", "replica", "da", "db"), None),
        P(("groups", "replica", "da", "db"), None),
        P(("da", "db"), "replica", None),
        P(("da", "db"), "replica", None),
    )
    return jax.shard_map(
        route,
        mesh=mesh,
        in_specs=placed,
        out_specs=(
            P(("groups", "replica", "da", "db"), None),
            P(("groups", "replica", "da", "db"), None),
            P(("groups", "da", "db"), "replica", None),
            P(("groups", "da", "db"), "replica", None),
        ),
        check_vma=False,
    )
```

profile of v0, /device:TPU:0, one launch (start us, length us, event | category | flops | bytes accessed | tf_op | source)
XLA Modules:
  0.0 83.8 jit_solution(10295013746316000547)
XLA Ops:
  0.6 81.7 %shard_map.93 = (bf16[128,1024]{1,0:T(8,128)(2,1)S(1)}, bf16[8,128]{1,0:T(8,128)(2,1)S(1)}, bf16[1,1024,768]{2,1,0:T(8,128)(2,1)S(1)}, bf16[1,384,1024]{2,1,0:T(8,128)(2,1)S(1)}) custom-call(bf16[128,1024]{1,0:T(8,128)(2,1)} %tok_hbm.1, bf16[128,1024]{1,0:T(8,128)(2,1)} %up_hbm.1, s32[8,128]{1,0:T(8,128)} %bitcast.3, bf16[8,128]{1,0:T(8,128)(2,1)} %bitcast.4, ...), custom_call_target="tpu_custom_call" | custom-call | tf_op jit(solution)/shard_map/pallas_call | solution.py:558
  82.3 1.5 %shard_map.94 = (bf16[128,1024]{1,0:T(8,128)(2,1)}, bf16[8,128]{1,0:T(8,128)(2,1)}, bf16[1,1024,768]{2,1,0:T(8,128)(2,1)}, bf16[1,384,1024]{2,1,0:T(8,128)(2,1)}) custom-call(bf16[128,1024]{1,0:T(8,128)(2,1)S(1)} %get-tuple-element.12.refs_0_, bf16[8,128]{1,0:T(8,128)(2,1)S(1)} %get-tuple-element.13.refs_1_, ...), custom_call_target="tpu_custom_call" | custom-call | tf_op jit(solution)/shard_map/pallas_call | solution.py:496
where the time goes:
time: 84 us; the launch traced here: 83.8 us
  Pallas kernels  83.2 us (99%)
    pallas_call x1, Pallas kernels, fused(): pl.pallas_call(functools.partial(fused_kernel, cols, depth, group), out_s...  81.7 us

commit v1 on v0

v1 whole, which is shorter than its diff:
```python
import functools

import jax
import jax.numpy as jnp
from jax import lax
from jax.experimental import pallas as pl
from jax.experimental.pallas import tpu as pltpu
from jax.sharding import PartitionSpec as P


CORES = 2
HALVES = 2
MESH = pl.DeviceIdType.MESH


def silu_parts(projected):
    sigmoid = jax.nn.sigmoid(projected)
    return (projected * sigmoid, sigmoid * (1.0 + projected * (1.0 - sigmoid)))


def body(tokens, grad_out, routes, gates, w_gate_up, w_down):
    local_tokens, features = tokens.shape
    top_count = routes.shape[1]
    hidden_units = w_gate_up.shape[2] // 2
    first_size = lax.axis_size("da")
    second_size = lax.axis_size("db")
    experts = first_size * second_size
    per_round = experts // top_count
    rounds = local_tokens // per_round
    expert_ids = lax.broadcasted_iota(jnp.int32, (1, 1, 1, experts), 3)
    matches = routes.reshape(rounds, per_round, top_count, 1) == expert_ids
    gate_values = gates.reshape(rounds, per_round, top_count, 1).astype(jnp.float32)
    gate_table = jnp.sum(jnp.where(matches, gate_values, 0.0), axis=(1, 2)).astype(jnp.bfloat16)
    chosen = jnp.any(matches, axis=2).astype(jnp.bfloat16)
    input_send = jnp.einsum(
        "rge,rgd->red",
        chosen,
        tokens.reshape(rounds, per_round, features),
        preferred_element_type=jnp.float32,
    ).astype(jnp.bfloat16)
    upstream_send = jnp.einsum(
        "rge,rgd->red",
        chosen,
        grad_out.reshape(rounds, per_round, features),
        preferred_element_type=jnp.float32,
    ).astype(jnp.bfloat16)
    input_recv, upstream_recv, gate_recv = (
        lax.all_to_all(input_send, ("da", "db"), split_axis=1, concat_axis=1, tiled=True),
        lax.all_to_all(upstream_send, ("da", "db"), split_axis=1, concat_axis=1, tiled=True),
        lax.all_to_all(gate_table, ("da", "db"), split_axis=1, concat_axis=1, tiled=True),
    )
    input_rows = input_recv.reshape(-1, features)
    upstream_rows = upstream_recv.reshape(-1, features)
    gate_rows = gate_recv.reshape(-1, 1).astype(jnp.float32)
    w_in, w_out = (
        lax.all_gather(w_gate_up[0], "replica", axis=0, tiled=True),
        lax.all_gather(w_down[0], "replica", axis=0, tiled=True),
    )
    projected = jnp.dot(input_rows, w_in, preferred_element_type=jnp.float32)
    back_raw = jnp.einsum("rd,fd->rf", upstream_rows, w_out, preferred_element_type=jnp.float32)
    gate_part = projected[:, :hidden_units]
    up_part = projected[:, hidden_units:]
    activated, derivative = silu_parts(gate_part)
    hidden = (activated * up_part).astype(jnp.bfloat16)
    gate_scores = jnp.sum(hidden.astype(jnp.float32) * back_raw, axis=1).astype(jnp.bfloat16)
    back_hidden = gate_rows * back_raw
    grad_projected = jnp.concatenate(
        [back_hidden * up_part * derivative, back_hidden * activated], axis=1
    ).astype(jnp.bfloat16)
    scaled_upstream = (gate_rows * upstream_rows.astype(jnp.float32)).astype(jnp.bfloat16)
    input_grads = jnp.einsum("rf,df->rd", grad_projected, w_in, preferred_element_type=jnp.float32)
    input_grads = input_grads.astype(jnp.bfloat16).reshape(rounds, experts, features)
    score_back = gate_scores.reshape(rounds, experts)
    returned, score_ret = (
        lax.all_to_all(input_grads, ("da", "db"), split_axis=1, concat_axis=1, tiled=True),
        lax.all_to_all(score_back, ("da", "db"), split_axis=1, concat_axis=1, tiled=True),
    )
    score_ret = score_ret.reshape(rounds, 1, 1, experts).astype(jnp.float32)
    token_grads = (
        jnp.einsum("rge,red->rgd", chosen, returned, preferred_element_type=jnp.float32)
        .astype(jnp.bfloat16)
        .reshape(local_tokens, features)
    )
    gate_grads = (
        jnp.sum(jnp.where(matches, score_ret, 0.0), axis=3)
        .astype(jnp.bfloat16)
        .reshape(local_tokens, top_count)
    )
    columns = input_rows
    grad_in = lax.psum_scatter(
        jnp.einsum("rd,rf->df", columns, grad_projected, preferred_element_type=jnp.float32).astype(
            jnp.bfloat16
        ),
        "replica",
        scatter_dimension=0,
        tiled=True,
    )
    columns = hidden
    grad_down = lax.psum_scatter(
        jnp.einsum(
            "rf,rd->fd", columns, scaled_upstream, preferred_element_type=jnp.float32
        ).astype(jnp.bfloat16),
        "replica",
        scatter_dimension=0,
        tiled=True,
    )
    return (token_grads, gate_grads, grad_in[None], grad_down[None])


def visit(j, z, n):
    m = jnp.minimum(z, n - 1 - z)
    near = z + (1 - 2 * (j % 2)) * ((j + 1) // 2)
    far = jnp.where(z < n - 1 - z, j, n - 1 - j)
    return jnp.where(j <= 2 * m, near, far)


def dot(a, b, dims):
    return lax.dot_general(a, b, (dims, ((), ())), preferred_element_type=jnp.float32)


def position(d, z, n):
    away = abs(d - z)
    if away <= min(z, n - 1 - z):
        return 2 * away - (1 if d < z else 0)
    return d if z < n - 1 - z else n - 1 - d


def relay_slots(n):
    last = 2 * n - 1

    def ready(z, d, h):
        k = position(d, z, n)
        k = last - k if h else k
        feeds = [u for u in (z - 1, z + 1) if 0 <= u < n and abs(u - d) == abs(z - d) + 1]
        return max([k + 1] + [ready(u, d, h) + 1 for u in feeds])

    table = []
    for z in range(n):
        row = [0] * (2 * n)
        for d in range(n):
            k = position(d, z, n)
            row[k] = ready(z, d, 0)
            row[last - k] = ready(z, d, 1)
        table.append(row)
    return table


def lag_words(n):
    return [sum((at - k - 1) * 8**k for k, at in enumerate(row)) for row in relay_slots(n)]


def fused_kernel(
    cols, depth, group,
    tok_hbm, up_hbm, routes_hbm, gates_hbm, win_hbm, wout_hbm,
    tg_ref, gg_ref, gin_ref, gdown_ref,
    routes_ref, gates_ref, tok, up, table, win, wout, xs, su, hid, gp, igs, igb, acc, cs, cr, rk, rx, scs, scr,
    load_sem, recv_sem, zup_sem, zdn_sem, x_sem, p_sem, igs_sem, igr_sem, cs_sem, cr_sem, rx_sem, scs_sem, scr_sem,
):
    da = lax.axis_index("da")
    z = lax.axis_index("db")
    x, c = da // CORES, da % CORES
    half, features = tok.shape[2], tok.shape[3]
    local = HALVES * half
    experts = table.shape[1]
    top = routes_ref.shape[0]
    rows = half // group
    ff = wout.shape[0]
    steps = HALVES * depth

    def slot(xx, zz, cc):
        return (xx * CORES + cc) * depth + zz

    me = slot(x, z, c)
    loads = []
    for h in range(HALVES):
        span = pl.ds(h * half, half)
        loads.append(pltpu.make_async_copy(tok_hbm.at[span], tok.at[me, h], load_sem.at[2 * h]))
        loads.append(pltpu.make_async_copy(up_hbm.at[span], up.at[me, h], load_sem.at[2 * h + 1]))
    loads += [
        pltpu.make_async_copy(win_hbm.at[0], win, load_sem.at[4]),
        pltpu.make_async_copy(wout_hbm.at[0], wout, load_sem.at[5]),
        pltpu.make_async_copy(routes_hbm, routes_ref, load_sem.at[6]),
        pltpu.make_async_copy(gates_hbm, gates_ref, load_sem.at[7]),
    ]
    barrier = pltpu.get_barrier_semaphore()
    count = cols * CORES * depth

    def greet(xx, zz, cc):
        pl.semaphore_signal(
            barrier, inc=1, device_id={"da": xx * CORES + cc, "db": zz}, device_id_type=MESH
        )

    @pl.when(z > 0)
    def _():
        greet(x, z - 1, c)

    @pl.when(z < depth - 1)
    def _():
        greet(x, z + 1, c)

    greet(1 - x, z, c)
    greet(x, z, 1 - c)
    for k in (6, 7, 0, 1, 2, 3, 4, 5):
        loads[k].start()

    loads[6].wait()
    loads[7].wait()
    routes = routes_ref[...]
    gates = gates_ref[...].astype(jnp.float32)
    ids = lax.broadcasted_iota(jnp.int32, (experts, local), 0)
    chart = jnp.zeros((experts, local), jnp.float32)
    for k in range(top):
        chart = chart + jnp.where(routes[k : k + 1] == ids, gates[k : k + 1], 0.0)
    table[me] = chart.astype(jnp.bfloat16)

    for k in range(4):
        loads[k].wait()
    pl.semaphore_wait(barrier, 2 + jnp.where(z > 0, 1, 0) + jnp.where(z < depth - 1, 1, 0))

    held = (tok, up)

    def send(src, dst, send_sem, recv, to_x, to_z, to_c):
        return pltpu.make_async_remote_copy(
            src_ref=src,
            dst_ref=dst,
            send_sem=send_sem,
            recv_sem=recv,
            device_id={"da": to_x * CORES + to_c, "db": to_z},
            device_id_type=MESH,
        )

    def relay(s, h, a, sem, to_x, to_z, to_c):
        ref = held[a].at[s, h]
        return send(ref, ref, sem, recv_sem.at[s, h, a], to_x, to_z, to_c)

    def relay_table(s, sem, to_x, to_z, to_c):
        ref = table.at[s]
        return send(ref, ref, sem, recv_sem.at[s, 0, 2], to_x, to_z, to_c)

    def both(s, zz, h, a, sems, act, to_x, to_z, to_c):
        act(relay(s, h, a, sems.at[zz, h, a], to_x, to_z, to_c))
        if a == 0:

            @pl.when(h == 0)
            def _():
                act(relay_table(s, sems.at[zz, 0, 2], to_x, to_z, to_c))

    def start(copy):
        copy.start()

    def wait_send(copy):
        copy.wait_send()

    def wait_recv(copy):
        copy.wait_recv()

    def step_of(i):
        j = jnp.minimum(i, steps - 1 - i)
        return visit(j, z, depth), jnp.where(i >= depth, 1, 0)

    def along_z(e, a):
        def one(reach, sign, sems):
            last = 2 * reach + 1
            k = jnp.minimum(e, last - e)
            h = jnp.where(e > reach, 1, 0)
            zz = z + sign * k
            s = slot(x, zz, c)

            @pl.when((e <= last) & (k > 0))
            def _():
                both(s, zz, h, a, p_sem.at[0], wait_recv, x, z, 1 - c)

            ahead = z - sign

            @pl.when((e <= last) & (ahead >= 0) & (ahead < depth))
            def _():
                both(s, zz, h, a, sems, start, x, ahead, c)

        one(depth - 1 - z, 1, zdn_sem)
        one(z, -1, zup_sem)

    def across(i, a):
        zz, h = step_of(i)
        s = slot(x, zz, c)
        if a == 0:

            @pl.when(i < steps - 1)
            def _():
                both(s, zz, h, a, x_sem, start, 1 - x, z, c)
        else:
            both(s, zz, h, a, x_sem, start, 1 - x, z, c)
        both(s, zz, h, a, p_sem.at[0], start, x, z, 1 - c)

    def from_across(i, a):
        zz, h = step_of(i)
        s = slot(1 - x, zz, c)
        both(s, zz, h, a, p_sem.at[1], wait_recv, x, z, 1 - c)
        both(s, zz, h, a, p_sem.at[1], start, x, z, 1 - c)

    def from_partner(i):
        zz, h = step_of(i)
        for xx in (x, 1 - x):
            for a in range(2):
                both(slot(xx, zz, 1 - c), zz, h, a, p_sem.at[0], wait_recv, x, z, 1 - c)

    def pick(s, e, h):
        chart_s = table[s].astype(jnp.float32)
        which = lax.broadcasted_iota(jnp.int32, chart_s.shape, 0) == e
        row = jnp.sum(jnp.where(which, chart_s, 0.0), axis=0, keepdims=True)
        row = jnp.where(h == 0, row[:, :half], row[:, half:])
        off = lax.broadcasted_iota(jnp.int32, (rows, half), 1) - group * lax.broadcasted_iota(
            jnp.int32, (rows, half), 0
        )
        hit = (off >= 0) & (off < group) & (row > 0.0)
        return jnp.where(hit, 1.0, 0.0), row

    def send_ig(q, k):
        return send(igs.at[k, q], igb.at[k, q, c], igs_sem.at[k, q], igr_sem.at[k, q], x, z, 1 - c)

    def send_score(s):
        return pltpu.make_async_remote_copy(
            src_ref=scs.at[s],
            dst_ref=scr.at[me],
            send_sem=scs_sem.at[s],
            recv_sem=scr_sem.at[me],
            device_id={"da": s // depth, "db": s % depth},
            device_id_type=MESH,
        )

    blocks = [(q, r) for q in range(cols) for r in range(CORES)]
    batch = len(blocks) * rows

    def compute(k):
        zz, h = step_of(k)
        base = pl.multiple_of(k * batch, batch)
        picks = []
        gate_cols = []
        for n, (q, r) in enumerate(blocks):
            s = slot((x + q) % cols, zz, (c + r) % CORES)
            chosen, row = pick(s, me, h)
            picks.append((s, chosen))
            gate_cols.append(jnp.sum(chosen * row, axis=1, keepdims=True))
            hot = chosen.astype(jnp.bfloat16)
            where = pl.ds(pl.multiple_of(base + n * rows, rows), rows)
            xs[where, :] = dot(hot, tok[s, h], ((1,), (0,))).astype(jnp.bfloat16)
            su[where, :] = dot(hot, up[s, h], ((1,), (0,))).astype(jnp.bfloat16)
        here = pl.ds(base, batch)
        gate = jnp.concatenate(gate_cols, axis=0)
        upstream = su[here, :]
        projected = dot(xs[here, :], win[...], ((1,), (0,)))
        back_raw = dot(upstream, wout[...], ((1,), (1,)))
        su[here, :] = (gate * upstream.astype(jnp.float32)).astype(jnp.bfloat16)
        gate_part, up_part = projected[:, :ff], projected[:, ff:]
        activated, derivative = silu_parts(gate_part)
        hidden = (activated * up_part).astype(jnp.bfloat16)
        hid[here, :] = hidden
        scores = jnp.sum(hidden.astype(jnp.float32) * back_raw, axis=1, keepdims=True)
        scores = scores.astype(jnp.bfloat16).astype(jnp.float32)
        back_hidden = gate * back_raw
        gp[here, :ff] = (back_hidden * up_part * derivative).astype(jnp.bfloat16)
        gp[here, ff:] = (back_hidden * activated).astype(jnp.bfloat16)
        grads = dot(gp[here, :], win[...], ((1,), (1,))).astype(jnp.bfloat16)
        for n, (q, r) in enumerate(blocks):
            piece = grads[n * rows : (n + 1) * rows]
            if r == 0:
                igb[k, q, c] = piece
            else:
                igs[k, q] = piece
                send_ig(q, k).start()
        for n, (q, r) in enumerate(blocks):
            s, chosen = picks[n]
            line = jnp.sum(chosen * scores[n * rows : (n + 1) * rows], axis=0, keepdims=True)
            rest = jnp.zeros_like(line)
            first = jnp.concatenate([line, rest], axis=1)
            second = jnp.concatenate([rest, line], axis=1)

            @pl.when(h == 0)
            def _():
                scs[s] = jnp.broadcast_to(first, scs.shape[1:])

            @pl.when(h == 1)
            def _():
                scs[s] = scs[s] + jnp.broadcast_to(second, scs.shape[1:])
                if q == 0 and r == 0:

                    @pl.when(zz == z)
                    def _():
                        scr[me] = scs[me]

                    @pl.when(zz != z)
                    def _():
                        send_score(s).start()
                else:
                    send_score(s).start()

    def chip_sum(k, q):
        zz, h = step_of(k)
        s = slot((x + q) % cols, zz, c)
        hot = jnp.concatenate([pick(s, slot(x, z, m), h)[0] for m in range(CORES)], axis=0)
        pair = igb[k, q].reshape(CORES * rows, features)
        return dot(hot.astype(jnp.bfloat16), pair, ((0,), (0,)))

    def send_sum(zz, h, q, side, to_z):
        return send(
            cs.at[zz, h, q], cr.at[side, zz, h, q], cs_sem.at[zz, h, q], cr_sem.at[side, zz, h, q], x, to_z, c
        )

    def send_across(h):
        return send(cs.at[z, h, 1], rx.at[h], cs_sem.at[z, h, 1], rx_sem.at[h], 1 - x, z, c)

    def pass_on(k, q):
        zz, h = step_of(k)
        send_ig(q, k).wait_recv()
        acc[...] = chip_sum(k, q)
        for side, ok in ((0, (zz <= z) & (z < depth - 1)), (1, (zz >= z) & (z > 0))):

            @pl.when(ok)
            def _():
                send_sum(zz, h, q, side, z).wait_recv()
                acc[...] += cr[side, zz, h, q].astype(jnp.float32)

        if q == 0:

            @pl.when(zz == z)
            def _():
                rk[h] = acc[...]

        @pl.when((zz != z) if q == 0 else True)
        def _():
            cs[zz, h, q] = acc[...].astype(jnp.bfloat16)

        @pl.when(zz < z)
        def _():
            send_sum(zz, h, q, 0, z - 1).start()

        @pl.when(zz > z)
        def _():
            send_sum(zz, h, q, 1, z + 1).start()

        if q == 1:

            @pl.when(zz == z)
            def _():
                send_across(h).start()

    words = lag_words(depth)
    word = jnp.int32(words[0])
    for k in range(1, depth):
        word = jnp.where(z == k, words[k], word)

    def pass_all(i, q):
        def one(k, left):
            @pl.when(k + 1 + left % 8 == i)
            def _():
                pass_on(k, q)

            return left // 8

        lax.fori_loop(0, jnp.minimum(i, steps), one, word)

    along_z(0, 0)
    across(0, 0)

    def step(i, carry):
        @pl.when(i < steps)
        def _():
            along_z(i, 1)
            across(i, 1)

        @pl.when(i == 0)
        def _():
            relay(me, 1, 0, x_sem.at[z, 1, 0], 1 - x, z, c).start()
            loads[4].wait()
            loads[5].wait()

        @pl.when(i >= 1)
        def _():
            from_across(i - 1, 1)
            pass_all(i - 1, 0)
            from_partner(i - 1)
            compute(i - 1)

        @pl.when(i + 1 < steps)
        def _():
            along_z(i + 1, 0)
            across(i + 1, 0)

        @pl.when(i < steps)
        def _():
            from_across(i, 0)

        @pl.when(i >= 1)
        def _():
            pass_all(i, 1)

        return carry

    lax.fori_loop(0, steps + 1, step, 0)
    pass_all(steps, 0)

    wide = min(features, 256)

    @pl.loop(0, features // wide)
    def _(t):
        at = pl.ds(pl.multiple_of(t * wide, wide), wide)
        gin_ref[0, at, :] = dot(xs[:, at], gp[...], ((0,), (0,))).astype(jnp.bfloat16)

    thin = 128

    @pl.loop(0, ff // thin)
    def _(t):
        at = pl.ds(pl.multiple_of(t * thin, thin), thin)
        gdown_ref[0, at, :] = dot(hid[:, at], su[...], ((0,), (0,))).astype(jnp.bfloat16)

    @pl.loop(1, count)
    def _(k):
        s = (me + k) % count
        pltpu.make_async_remote_copy(
            src_ref=scs.at[s],
            dst_ref=scr.at[s],
            send_sem=scs_sem.at[s],
            recv_sem=scr_sem.at[s],
            device_id={"da": s // depth, "db": s % depth},
            device_id_type=MESH,
        ).wait()

    scores = scr[:, 0, :]
    place = lax.broadcasted_iota(jnp.int32, (top, local), 0)
    gate_grads = jnp.zeros((top, local), jnp.float32)
    for k in range(top):
        value = jnp.sum(jnp.where(routes[k : k + 1] == ids, scores, 0.0), axis=0, keepdims=True)
        gate_grads = jnp.where(place == k, value, gate_grads)
    gg_ref[...] = gate_grads.astype(jnp.bfloat16)

    for h in range(HALVES):
        send_across(h).wait_recv()
        tg_ref[pl.ds(h * half, half), :] = (rk[h] + rx[h].astype(jnp.float32)).astype(jnp.bfloat16)

    def drain(k, carry):
        zz, h = k // HALVES, k % HALVES
        s = slot(x, zz, c)
        for a in range(2):

            @pl.when((zz <= z) & (z < depth - 1))
            def _():
                both(s, zz, h, a, zup_sem, wait_send, x, z + 1, c)

            @pl.when((zz >= z) & (z > 0))
            def _():
                both(s, zz, h, a, zdn_sem, wait_send, x, z - 1, c)

            both(s, zz, h, a, x_sem, wait_send, 1 - x, z, c)
            for o in range(2):
                both(s, zz, h, a, p_sem.at[o], wait_send, x, z, 1 - c)
        for q in range(cols):
            send_ig(q, k).wait_send()
        send(cs.at[zz, h, 1], rx.at[h], cs_sem.at[zz, h, 1], rx_sem.at[h], 1 - x, z, c).wait_send()

        @pl.when(zz != z)
        def _():
            send(cs.at[zz, h, 0], rx.at[h], cs_sem.at[zz, h, 0], rx_sem.at[h], 1 - x, z, c).wait_send()

        return carry

    lax.fori_loop(0, steps, drain, 0)


def store_kernel(*refs):
    count = len(refs) // 2
    sems = refs[-1]
    copies = [
        pltpu.make_async_copy(refs[k], refs[count + k], sems.at[k]) for k in range(count)
    ]
    for one in copies:
        one.start()
    for one in copies:
        one.wait()


def store(*arrays):
    anywhere = pl.BlockSpec(memory_space=pl.ANY)
    return pl.pallas_call(
        store_kernel,
        out_shape=tuple(jax.ShapeDtypeStruct(a.shape, a.dtype) for a in arrays),
        in_specs=[pl.BlockSpec(memory_space=pltpu.VMEM)] * len(arrays),
        out_specs=(pl.BlockSpec(memory_space=pltpu.HBM),) * len(arrays),
        scratch_shapes=[pltpu.SemaphoreType.DMA((len(arrays),))],
        compiler_params=pltpu.CompilerParams(vmem_limit_bytes=8 * 2**20),
    )(*arrays)


def fused(tokens, grad_out, routes, gates, w_gate_up, w_down):
    first_size, depth = lax.axis_size("da"), lax.axis_size("db")
    cols = first_size // CORES
    experts = first_size * depth
    local, features = tokens.shape
    top = routes.shape[1]
    group = experts // top
    ff = w_down.shape[1]
    bf, f32 = jnp.bfloat16, jnp.float32
    half = local // HALVES
    rows = half // group
    steps = HALVES * depth
    total = rows * experts * HALVES
    dma = pltpu.SemaphoreType.DMA
    scratch = [
        pltpu.VMEM((top, local), routes.dtype),
        pltpu.VMEM((top, local), gates.dtype),
        pltpu.VMEM((experts, HALVES, half, features), bf),
        pltpu.VMEM((experts, HALVES, half, features), bf),
        pltpu.VMEM((experts, experts, local), bf),
        pltpu.VMEM((features, 2 * ff), bf),
        pltpu.VMEM((ff, features), bf),
        pltpu.VMEM((total, features), bf),
        pltpu.VMEM((total, features), bf),
        pltpu.VMEM((total, ff), bf),
        pltpu.VMEM((total, 2 * ff), bf),
        pltpu.VMEM((steps, cols, rows, features), bf),
        pltpu.VMEM((steps, cols, CORES, rows, features), bf),
        pltpu.VMEM((half, features), f32),
        pltpu.VMEM((depth, HALVES, cols, half, features), bf),
        pltpu.VMEM((2, depth, HALVES, cols, half, features), bf),
        pltpu.VMEM((HALVES, half, features), f32),
        pltpu.VMEM((HALVES, half, features), bf),
        pltpu.VMEM((experts, 8, local), f32),
        pltpu.VMEM((experts, 8, local), f32),
        dma((8,)),
        dma((experts, HALVES, 3)),
        dma((depth, HALVES, 3)),
        dma((depth, HALVES, 3)),
        dma((depth, HALVES, 3)),
        dma((cols, depth, HALVES, 3)),
        dma((steps, cols)),
        dma((steps, cols)),
        dma((depth, HALVES, cols)),
        dma((2, depth, HALVES, cols)),
        dma((HALVES,)),
        dma((experts,)),
        dma((experts,)),
    ]
    vmem = pl.BlockSpec(memory_space=pltpu.VMEM)
    hbm = pl.BlockSpec(memory_space=pltpu.HBM)
    token_grads, gate_grads, grad_in, grad_down = pl.pallas_call(
        functools.partial(fused_kernel, cols, depth, group),
        out_shape=(
            jax.ShapeDtypeStruct((local, features), bf),
            jax.ShapeDtypeStruct((top, local), bf),
            jax.ShapeDtypeStruct(w_gate_up.shape, bf),
            jax.ShapeDtypeStruct(w_down.shape, bf),
        ),
        in_specs=[hbm] * 6,
        out_specs=(vmem, vmem, vmem, vmem),
        scratch_shapes=scratch,
        compiler_params=pltpu.CompilerParams(
            collective_id=0, has_side_effects=True, vmem_limit_bytes=44 * 2**20
        ),
    )(
        *(
            pltpu.with_memory_space_constraint(a, pltpu.HBM)
            for a in (tokens, grad_out, routes.T, gates.T, w_gate_up, w_down)
        )
    )
    token_grads, gate_grads, grad_in, grad_down = store(token_grads, gate_grads, grad_in, grad_down)
    return token_grads, gate_grads.T, grad_in, grad_down


def fits(tokens, routes, w_down):
    first_size = lax.axis_size("da")
    experts = first_size * lax.axis_size("db")
    local, features = tokens.shape
    group = experts // routes.shape[1]
    held = 2 * experts * local * features * 2
    return (
        lax.axis_size("replica") == 1
        and first_size % CORES == 0
        and first_size == 2 * CORES
        and 2 * 3 * lax.axis_size("db") <= 30
        and held <= 16 * 2**20
        and local == 128
        and experts <= local
        and (local // (HALVES * group)) % 16 == 0
        and w_down.shape[1] % 128 == 0
    )


def route(*arrays):
    if fits(arrays[0], arrays[2], arrays[5]):
        return fused(*arrays)
    return body(*arrays)


def solution(mesh):
    placed = (
        P(("groups", "replica", "da", "db"), None),
        P(("groups", "replica", "da", "db"), None),
        P(("groups", "replica", "da", "db"), None),
        P(("groups", "replica", "da", "db"), None),
        P(("da", "db"), "replica", None),
        P(("da", "db"), "replica", None),
    )
    return jax.shard_map(
        route,
        mesh=mesh,
        in_specs=placed,
        out_specs=(
            P(("groups", "replica", "da", "db"), None),
            P(("groups", "replica", "da", "db"), None),
            P(("groups", "da", "db"), "replica", None),
            P(("groups", "da", "db"), "replica", None),
        ),
        check_vma=False,
    )
```

time: 84 us -> 72.7 us (0.87)
  Pallas kernels: 83.2 us -> 71.8 us
    pallas_call x1, Pallas kernels: 81.7 us -> 70.3 us  [fused(): pl.pallas_call(functools.partial(fused_kernel, cols, depth, group), out_s...]
where the time goes in v1:
time: 72.7 us; the launch traced here: 72.5 us
  Pallas kernels  71.8 us (99%)
    pallas_call x1, Pallas kernels, fused(): pl.pallas_call(functools.partial(fused_kernel, cols, depth, group), out_s...  70.3 us
    pallas_call x1, Pallas kernels, store(): pl.pallas_call(store_kernel, out_shape=tuple((jax.ShapeDtypeStruct(a.shap...  1.53 us

profile of v1, /device:TPU:0, one launch (start us, length us, event | category | flops | bytes accessed | tf_op | source)
XLA Modules:
  0.0 72.5 jit_solution(1604452437463047725)
XLA Ops:
  0.6 70.3 %shard_map.93 = (bf16[128,1024]{1,0:T(8,128)(2,1)S(1)}, bf16[8,128]{1,0:T(8,128)(2,1)S(1)}, bf16[1,1024,768]{2,1,0:T(8,128)(2,1)S(1)}, bf16[1,384,1024]{2,1,0:T(8,128)(2,1)S(1)}) custom-call(bf16[128,1024]{1,0:T(8,128)(2,1)} %tok_hbm.1, bf16[128,1024]{1,0:T(8,128)(2,1)} %up_hbm.1, s32[8,128]{1,0:T(8,128)} %bitcast.3, bf16[8,128]{1,0:T(8,128)(2,1)} %bitcast.4, ...), custom_call_target="tpu_custom_call" | custom-call | tf_op jit(solution)/shard_map/pallas_call | solution.py:643
  70.9 1.5 %shard_map.94 = (bf16[128,1024]{1,0:T(8,128)(2,1)}, bf16[8,128]{1,0:T(8,128)(2,1)}, bf16[1,1024,768]{2,1,0:T(8,128)(2,1)}, bf16[1,384,1024]{2,1,0:T(8,128)(2,1)}) custom-call(bf16[128,1024]{1,0:T(8,128)(2,1)S(1)} %get-tuple-element.12.refs_0_, bf16[8,128]{1,0:T(8,128)(2,1)S(1)} %get-tuple-element.13.refs_1_, ...), custom_call_target="tpu_custom_call" | custom-call | tf_op jit(solution)/shard_map/pallas_call | solution.py:582

commit v2 on v1

--- a/solution.py
+++ b/solution.py
@@ -132,7 +132,7 @@
         k = position(d, z, n)
         k = last - k if h else k
         feeds = [u for u in (z - 1, z + 1) if 0 <= u < n and abs(u - d) == abs(z - d) + 1]
-        return max([k + 1] + [ready(u, d, h) + 1 for u in feeds])
+        return max([k + 2] + [ready(u, d, h) + 1 for u in feeds])
 
     table = []
     for z in range(n):
@@ -146,7 +146,7 @@
 
 
 def lag_words(n):
-    return [sum((at - k - 1) * 8**k for k, at in enumerate(row)) for row in relay_slots(n)]
+    return [sum((at - k - 2) * 8**k for k, at in enumerate(row)) for row in relay_slots(n)]
 
 
 def fused_kernel(
@@ -154,7 +154,7 @@
     tok_hbm, up_hbm, routes_hbm, gates_hbm, win_hbm, wout_hbm,
     tg_ref, gg_ref, gin_ref, gdown_ref,
     routes_ref, gates_ref, tok, up, table, win, wout, xs, su, hid, gp, igs, igb, acc, cs, cr, rk, rx, scs, scr,
-    load_sem, recv_sem, zup_sem, zdn_sem, x_sem, p_sem, igs_sem, igr_sem, cs_sem, cr_sem, rx_sem, scs_sem, scr_sem,
+    load_sem, recv_sem, chart_sem, near_sem, near_chart_sem, igr_sem, cr_sem, rx_sem, scr_sem, sent_sem,
 ):
     da = lax.axis_index("da")
     z = lax.axis_index("db")
@@ -174,14 +174,17 @@
     loads = []
     for h in range(HALVES):
         span = pl.ds(h * half, half)
-        loads.append(pltpu.make_async_copy(tok_hbm.at[span], tok.at[me, h], load_sem.at[2 * h]))
-        loads.append(pltpu.make_async_copy(up_hbm.at[span], up.at[me, h], load_sem.at[2 * h + 1]))
+        loads.append(pltpu.make_async_copy(tok_hbm.at[span], tok.at[me, h], load_sem.at[0]))
+        loads.append(pltpu.make_async_copy(up_hbm.at[span], up.at[me, h], load_sem.at[0]))
     loads += [
-        pltpu.make_async_copy(win_hbm.at[0], win, load_sem.at[4]),
-        pltpu.make_async_copy(wout_hbm.at[0], wout, load_sem.at[5]),
-        pltpu.make_async_copy(routes_hbm, routes_ref, load_sem.at[6]),
-        pltpu.make_async_copy(gates_hbm, gates_ref, load_sem.at[7]),
+        pltpu.make_async_copy(win_hbm.at[0], win, load_sem.at[1]),
+        pltpu.make_async_copy(wout_hbm.at[0], wout, load_sem.at[2]),
+        pltpu.make_async_copy(routes_hbm, routes_ref, load_sem.at[3]),
+        pltpu.make_async_copy(gates_hbm, gates_ref, load_sem.at[4]),
     ]
+    def settle(view, sem):
+        pltpu.make_async_copy(view, view, sem).wait()
+
     barrier = pltpu.get_barrier_semaphore()
     count = cols * CORES * depth
 
@@ -213,8 +216,7 @@
         chart = chart + jnp.where(routes[k : k + 1] == ids, gates[k : k + 1], 0.0)
     table[me] = chart.astype(jnp.bfloat16)
 
-    for k in range(4):
-        loads[k].wait()
+    settle(tok.at[pl.ds(0, CORES)], load_sem.at[0])
     pl.semaphore_wait(barrier, 2 + jnp.where(z > 0, 1, 0) + jnp.where(z < depth - 1, 1, 0))
 
     held = (tok, up)
@@ -229,79 +231,66 @@
             device_id_type=MESH,
         )
 
-    def relay(s, h, a, sem, to_x, to_z, to_c):
-        ref = held[a].at[s, h]
-        return send(ref, ref, sem, recv_sem.at[s, h, a], to_x, to_z, to_c)
-
-    def relay_table(s, sem, to_x, to_z, to_c):
-        ref = table.at[s]
-        return send(ref, ref, sem, recv_sem.at[s, 0, 2], to_x, to_z, to_c)
-
-    def both(s, zz, h, a, sems, act, to_x, to_z, to_c):
-        act(relay(s, h, a, sems.at[zz, h, a], to_x, to_z, to_c))
-        if a == 0:
-
-            @pl.when(h == 0)
-            def _():
-                act(relay_table(s, sems.at[zz, 0, 2], to_x, to_z, to_c))
-
     def start(copy):
         copy.start()
 
-    def wait_send(copy):
-        copy.wait_send()
-
     def wait_recv(copy):
         copy.wait_recv()
+
+    def both(xx, zz, h, a, way, act, to_x, to_z, to_c, near=None):
+        s = slot(xx, zz, c)
+        ref = held[a].at[s, h]
+        landed = recv_sem.at[xx, zz, h, a] if near is None else near_sem.at[near]
+        act(send(ref, ref, sent_sem.at[way], landed, to_x, to_z, to_c))
+        if a == 0:
+
+            @pl.when(h == 0)
+            def _():
+                ref = table.at[s]
+                landed = chart_sem.at[xx, zz] if near is None else near_chart_sem.at[zz]
+                act(send(ref, ref, sent_sem.at[3 + (way > 0)], landed, to_x, to_z, to_c))
 
     def step_of(i):
         j = jnp.minimum(i, steps - 1 - i)
         return visit(j, z, depth), jnp.where(i >= depth, 1, 0)
 
     def along_z(e, a):
-        def one(reach, sign, sems):
+        def one(reach, sign):
             last = 2 * reach + 1
             k = jnp.minimum(e, last - e)
             h = jnp.where(e > reach, 1, 0)
             zz = z + sign * k
-            s = slot(x, zz, c)
 
             @pl.when((e <= last) & (k > 0))
             def _():
-                both(s, zz, h, a, p_sem.at[0], wait_recv, x, z, 1 - c)
+                both(x, zz, h, a, 0, wait_recv, x, z, 1 - c)
 
             ahead = z - sign
 
             @pl.when((e <= last) & (ahead >= 0) & (ahead < depth))
             def _():
-                both(s, zz, h, a, sems, start, x, ahead, c)
-
-        one(depth - 1 - z, 1, zdn_sem)
-        one(z, -1, zup_sem)
+                both(x, zz, h, a, 0, start, x, ahead, c)
+
+        one(depth - 1 - z, 1)
+        one(z, -1)
 
     def across(i, a):
         zz, h = step_of(i)
-        s = slot(x, zz, c)
-        if a == 0:
-
-            @pl.when(i < steps - 1)
-            def _():
-                both(s, zz, h, a, x_sem, start, 1 - x, z, c)
-        else:
-            both(s, zz, h, a, x_sem, start, 1 - x, z, c)
-        both(s, zz, h, a, p_sem.at[0], start, x, z, 1 - c)
+        both(x, zz, h, a, 1, start, 1 - x, z, c)
+        both(x, zz, h, a, 2, start, x, z, 1 - c, near=i)
 
     def from_across(i, a):
         zz, h = step_of(i)
-        s = slot(1 - x, zz, c)
-        both(s, zz, h, a, p_sem.at[1], wait_recv, x, z, 1 - c)
-        both(s, zz, h, a, p_sem.at[1], start, x, z, 1 - c)
+        both(1 - x, zz, h, a, 1, wait_recv, 1 - x, z, c)
+        both(1 - x, zz, h, a, 2, start, x, z, 1 - c, near=i)
 
     def from_partner(i):
         zz, h = step_of(i)
-        for xx in (x, 1 - x):
-            for a in range(2):
-                both(slot(xx, zz, 1 - c), zz, h, a, p_sem.at[0], wait_recv, x, z, 1 - c)
+        settle(tok.at[pl.ds(0, cols)], near_sem.at[i])
+
+        @pl.when(h == 0)
+        def _():
+            settle(table.at[pl.ds(0, cols)], near_chart_sem.at[zz])
 
     def pick(s, e, h):
         chart_s = table[s].astype(jnp.float32)
@@ -315,14 +304,14 @@
         return jnp.where(hit, 1.0, 0.0), row
 
     def send_ig(q, k):
-        return send(igs.at[k, q], igb.at[k, q, c], igs_sem.at[k, q], igr_sem.at[k, q], x, z, 1 - c)
+        return send(igs.at[k, q], igb.at[k, q, c], sent_sem.at[5], igr_sem.at[k, q], x, z, 1 - c)
 
     def send_score(s):
         return pltpu.make_async_remote_copy(
             src_ref=scs.at[s],
             dst_ref=scr.at[me],
-            send_sem=scs_sem.at[s],
-            recv_sem=scr_sem.at[me],
+            send_sem=sent_sem.at[7],
+            recv_sem=scr_sem.at[0],
             device_id={"da": s // depth, "db": s % depth},
             device_id_type=MESH,
         )
@@ -401,12 +390,12 @@
         return dot(hot.astype(jnp.bfloat16), pair, ((0,), (0,)))
 
     def send_sum(zz, h, q, side, to_z):
-        return send(
-            cs.at[zz, h, q], cr.at[side, zz, h, q], cs_sem.at[zz, h, q], cr_sem.at[side, zz, h, q], x, to_z, c
-        )
+        place = jnp.where((zz == to_z) & (side == 1), depth, zz)
+        landed = cr.at[place, h, q]
+        return send(cs.at[zz, h, q], landed, sent_sem.at[6], cr_sem.at[place, h, q], x, to_z, c)
 
     def send_across(h):
-        return send(cs.at[z, h, 1], rx.at[h], cs_sem.at[z, h, 1], rx_sem.at[h], 1 - x, z, c)
+        return send(cs.at[z, h, 1], rx.at[h], sent_sem.at[6], rx_sem.at[h], 1 - x, z, c)
 
     def pass_on(k, q):
         zz, h = step_of(k)
@@ -417,7 +406,8 @@
             @pl.when(ok)
             def _():
                 send_sum(zz, h, q, side, z).wait_recv()
-                acc[...] += cr[side, zz, h, q].astype(jnp.float32)
+                place = jnp.where((zz == z) & (side == 1), depth, zz)
+                acc[...] += cr[place, h, q].astype(jnp.float32)
 
         if q == 0:
 
@@ -448,15 +438,30 @@
     for k in range(1, depth):
         word = jnp.where(z == k, words[k], word)
 
-    def pass_all(i, q):
+    edge = (z == 0) | (z == depth - 1)
+
+    def pass_all(i, q, which=None):
         def one(k, left):
-            @pl.when(k + 1 + left % 8 == i)
+            due = k + 2 + left % 8 == i
+            if which is not None:
+                due = due & which(step_of(k)[0] == z)
+
+            @pl.when(due)
             def _():
                 pass_on(k, q)
 
             return left // 8
 
-        lax.fori_loop(0, jnp.minimum(i, steps), one, word)
+        lax.fori_loop(0, jnp.minimum(i - 1, steps), one, word)
+
+    def head(home):
+        return edge & jnp.logical_not(home)
+
+    def inner(home):
+        return jnp.logical_not(head(home))
+
+    def away(home):
+        return jnp.logical_not(home)
 
     along_z(0, 0)
     across(0, 0)
@@ -469,14 +474,28 @@
 
         @pl.when(i == 0)
         def _():
-            relay(me, 1, 0, x_sem.at[z, 1, 0], 1 - x, z, c).start()
             loads[4].wait()
             loads[5].wait()
 
+        @pl.when(i == steps)
+        def _():
+            pass_all(i, 1)
+
         @pl.when(i >= 1)
         def _():
             from_across(i - 1, 1)
-            pass_all(i - 1, 0)
+
+        @pl.when((i >= 2) & (i < steps))
+        def _():
+            pass_all(i, 1)
+            pass_all(i, 0, head)
+
+        @pl.when(i == steps)
+        def _():
+            pass_all(i, 0, away)
+
+        @pl.when(i >= 1)
+        def _():
             from_partner(i - 1)
             compute(i - 1)
 
@@ -485,18 +504,18 @@
             along_z(i + 1, 0)
             across(i + 1, 0)
 
+        @pl.when((i >= 2) & (i < steps))
+        def _():
+            pass_all(i, 0, inner)
+
         @pl.when(i < steps)
         def _():
             from_across(i, 0)
 
-        @pl.when(i >= 1)
-        def _():
-            pass_all(i, 1)
-
         return carry
 
     lax.fori_loop(0, steps + 1, step, 0)
-    pass_all(steps, 0)
+    pass_all(steps + 1, 1)
 
     wide = min(features, 256)
 
@@ -512,18 +531,12 @@
         at = pl.ds(pl.multiple_of(t * thin, thin), thin)
         gdown_ref[0, at, :] = dot(hid[:, at], su[...], ((0,), (0,))).astype(jnp.bfloat16)
 
-    @pl.loop(1, count)
-    def _(k):
-        s = (me + k) % count
-        pltpu.make_async_remote_copy(
-            src_ref=scs.at[s],
-            dst_ref=scr.at[s],
-            send_sem=scs_sem.at[s],
-            recv_sem=scr_sem.at[s],
-            device_id={"da": s // depth, "db": s % depth},
-            device_id_type=MESH,
-        ).wait()
-
+    def home(is_home):
+        return is_home
+
+    pass_all(steps, 0, home)
+    pass_all(steps + 1, 0)
+    settle(scr.at[pl.ds(0, count - 1)], scr_sem.at[0])
     scores = scr[:, 0, :]
     place = lax.broadcasted_iota(jnp.int32, (top, local), 0)
     gate_grads = jnp.zeros((top, local), jnp.float32)
@@ -536,33 +549,20 @@
         send_across(h).wait_recv()
         tg_ref[pl.ds(h * half, half), :] = (rk[h] + rx[h].astype(jnp.float32)).astype(jnp.bfloat16)
 
-    def drain(k, carry):
-        zz, h = k // HALVES, k % HALVES
-        s = slot(x, zz, c)
-        for a in range(2):
-
-            @pl.when((zz <= z) & (z < depth - 1))
-            def _():
-                both(s, zz, h, a, zup_sem, wait_send, x, z + 1, c)
-
-            @pl.when((zz >= z) & (z > 0))
-            def _():
-                both(s, zz, h, a, zdn_sem, wait_send, x, z - 1, c)
-
-            both(s, zz, h, a, x_sem, wait_send, 1 - x, z, c)
-            for o in range(2):
-                both(s, zz, h, a, p_sem.at[o], wait_send, x, z, 1 - c)
-        for q in range(cols):
-            send_ig(q, k).wait_send()
-        send(cs.at[zz, h, 1], rx.at[h], cs_sem.at[zz, h, 1], rx_sem.at[h], 1 - x, z, c).wait_send()
-
-        @pl.when(zz != z)
-        def _():
-            send(cs.at[zz, h, 0], rx.at[h], cs_sem.at[zz, h, 0], rx_sem.at[h], 1 - x, z, c).wait_send()
-
-        return carry
-
-    lax.fori_loop(0, steps, drain, 0)
+    for at in range(depth):
+        sent = (depth - at if at > 0 else 0) + (at + 1 if at < depth - 1 else 0)
+
+        @pl.when(z == at)
+        def _():
+            settle(tok.at[pl.ds(0, 2 * sent)], sent_sem.at[0])
+            settle(table.at[pl.ds(0, sent)], sent_sem.at[3])
+
+    settle(tok.at[pl.ds(0, 2 * depth)], sent_sem.at[1])
+    settle(tok, sent_sem.at[2])
+    settle(table.at[pl.ds(0, 3 * depth)], sent_sem.at[4])
+    settle(igs, sent_sem.at[5])
+    settle(tok.at[pl.ds(0, depth * cols - 1)], sent_sem.at[6])
+    settle(scs.at[pl.ds(0, count - 1)], sent_sem.at[7])
 
 
 def store_kernel(*refs):
@@ -619,24 +619,21 @@
         pltpu.VMEM((steps, cols, CORES, rows, features), bf),
         pltpu.VMEM((half, features), f32),
         pltpu.VMEM((depth, HALVES, cols, half, features), bf),
-        pltpu.VMEM((2, depth, HALVES, cols, half, features), bf),
+        pltpu.VMEM((depth + 1, HALVES, cols, half, features), bf),
         pltpu.VMEM((HALVES, half, features), f32),
         pltpu.VMEM((HALVES, half, features), bf),
         pltpu.VMEM((experts, 8, local), f32),
         pltpu.VMEM((experts, 8, local), f32),
+        dma((5,)),
+        dma((cols, depth, HALVES, 2)),
+        dma((cols, depth)),
+        dma((steps,)),
+        dma((depth,)),
+        dma((steps, cols)),
+        dma((depth + 1, HALVES, cols)),
+        dma((HALVES,)),
+        dma((1,)),
         dma((8,)),
-        dma((experts, HALVES, 3)),
-        dma((depth, HALVES, 3)),
-        dma((depth, HALVES, 3)),
-        dma((depth, HALVES, 3)),
-        dma((cols, depth, HALVES, 3)),
-        dma((steps, cols)),
-        dma((steps, cols)),
-        dma((depth, HALVES, cols)),
-        dma((2, depth, HALVES, cols)),
-        dma((HALVES,)),
-        dma((experts,)),
-        dma((experts,)),
     ]
     vmem = pl.BlockSpec(memory_space=pltpu.VMEM)
     hbm = pl.BlockSpec(memory_space=pltpu.HBM)
@@ -678,6 +675,7 @@
         and held <= 16 * 2**20
         and local == 128
         and experts <= local
+        and max(map(max, relay_slots(lax.axis_size("db")))) == HALVES * lax.axis_size("db") + 1
         and (local // (HALVES * group)) % 16 == 0
         and w_down.shape[1] % 128 == 0
     )

time: 72.7 us -> 66.3 us (0.912)
  Pallas kernels: 71.8 us -> 65.5 us
    pallas_call x1, Pallas kernels: 70.3 us -> 63.9 us  [fused(): pl.pallas_call(functools.partial(fused_kernel, cols, depth, group), out_s...]
where the time goes in v2:
time: 66.3 us; the launch traced here: 66.1 us
  Pallas kernels  65.5 us (99%)
    pallas_call x1, Pallas kernels, fused(): pl.pallas_call(functools.partial(fused_kernel, cols, depth, group), out_s...  63.9 us
    pallas_call x1, Pallas kernels, store(): pl.pallas_call(store_kernel, out_shape=tuple((jax.ShapeDtypeStruct(a.shap...  1.53 us

profile of v2, /device:TPU:0, one launch (start us, length us, event | category | flops | bytes accessed | tf_op | source)
XLA Modules:
  0.0 66.1 jit_solution(1469446812629237425)
XLA Ops:
  0.6 63.9 %shard_map.93 = (bf16[128,1024]{1,0:T(8,128)(2,1)S(1)}, bf16[8,128]{1,0:T(8,128)(2,1)S(1)}, bf16[1,1024,768]{2,1,0:T(8,128)(2,1)S(1)}, bf16[1,384,1024]{2,1,0:T(8,128)(2,1)S(1)}) custom-call(bf16[128,1024]{1,0:T(8,128)(2,1)} %tok_hbm.1, bf16[128,1024]{1,0:T(8,128)(2,1)} %up_hbm.1, s32[8,128]{1,0:T(8,128)} %bitcast.3, bf16[8,128]{1,0:T(8,128)(2,1)} %bitcast.4, ...), custom_call_target="tpu_custom_call" | custom-call | tf_op jit(solution)/shard_map/pallas_call | solution.py:640
  64.6 1.5 %shard_map.94 = (bf16[128,1024]{1,0:T(8,128)(2,1)}, bf16[8,128]{1,0:T(8,128)(2,1)}, bf16[1,1024,768]{2,1,0:T(8,128)(2,1)}, bf16[1,384,1024]{2,1,0:T(8,128)(2,1)}) custom-call(bf16[128,1024]{1,0:T(8,128)(2,1)S(1)} %get-tuple-element.12.refs_0_, bf16[8,128]{1,0:T(8,128)(2,1)S(1)} %get-tuple-element.13.refs_1_, ...), custom_call_target="tpu_custom_call" | custom-call | tf_op jit(solution)/shard_map/pallas_call | solution.py:582

commit v3 on v2

--- a/solution.py
+++ b/solution.py
@@ -146,7 +146,7 @@
 
 
 def lag_words(n):
-    return [sum((at - k - 2) * 8**k for k, at in enumerate(row)) for row in relay_slots(n)]
+    return [sum((at - k - 2) * 8 ** (2 * n - 1 - k) for k, at in enumerate(row)) for row in relay_slots(n)]
 
 
 def fused_kernel(
@@ -439,12 +439,12 @@
         word = jnp.where(z == k, words[k], word)
 
     edge = (z == 0) | (z == depth - 1)
-
-    def pass_all(i, q, which=None):
-        def one(k, left):
-            due = k + 2 + left % 8 == i
-            if which is not None:
-                due = due & which(step_of(k)[0] == z)
+    inner = jnp.logical_not(edge)
+
+    def pass_all(i, q):
+        def one(j, left):
+            k = steps - 1 - j
+            due = (k + 2 + left % 8 == i) & (j > 0)
 
             @pl.when(due)
             def _():
@@ -452,16 +452,7 @@
 
             return left // 8
 
-        lax.fori_loop(0, jnp.minimum(i - 1, steps), one, word)
-
-    def head(home):
-        return edge & jnp.logical_not(home)
-
-    def inner(home):
-        return jnp.logical_not(head(home))
-
-    def away(home):
-        return jnp.logical_not(home)
+        lax.fori_loop(0, steps - 1, one, word)
 
     along_z(0, 0)
     across(0, 0)
@@ -477,22 +468,21 @@
             loads[4].wait()
             loads[5].wait()
 
+        @pl.when(inner & (i >= 2))
+        def _():
+            pass_all(i, 1)
+
+        @pl.when(i >= 1)
+        def _():
+            from_across(i - 1, 1)
+
+        @pl.when(inner & (i >= 2) & (i < steps))
+        def _():
+            pass_all(i, 0)
+
         @pl.when(i == steps)
         def _():
-            pass_all(i, 1)
-
-        @pl.when(i >= 1)
-        def _():
-            from_across(i - 1, 1)
-
-        @pl.when((i >= 2) & (i < steps))
-        def _():
-            pass_all(i, 1)
-            pass_all(i, 0, head)
-
-        @pl.when(i == steps)
-        def _():
-            pass_all(i, 0, away)
+            pass_on(0, 1)
 
         @pl.when(i >= 1)
         def _():
@@ -504,18 +494,23 @@
             along_z(i + 1, 0)
             across(i + 1, 0)
 
-        @pl.when((i >= 2) & (i < steps))
-        def _():
-            pass_all(i, 0, inner)
-
         @pl.when(i < steps)
         def _():
             from_across(i, 0)
 
+        @pl.when(edge & (i >= 1) & (i < steps))
+        def _():
+            pass_all(i + 1, 1)
+            pass_all(i + 1, 0)
+
         return carry
 
     lax.fori_loop(0, steps + 1, step, 0)
-    pass_all(steps + 1, 1)
+    @pl.when(inner)
+    def _():
+        pass_all(steps, 0)
+
+    pass_on(steps - 1, 1)
 
     wide = min(features, 256)
 
@@ -531,11 +526,8 @@
         at = pl.ds(pl.multiple_of(t * thin, thin), thin)
         gdown_ref[0, at, :] = dot(hid[:, at], su[...], ((0,), (0,))).astype(jnp.bfloat16)
 
-    def home(is_home):
-        return is_home
-
-    pass_all(steps, 0, home)
-    pass_all(steps + 1, 0)
+    pass_on(0, 0)
+    pass_on(steps - 1, 0)
     settle(scr.at[pl.ds(0, count - 1)], scr_sem.at[0])
     scores = scr[:, 0, :]
     place = lax.broadcasted_iota(jnp.int32, (top, local), 0)

time: 66.3 us -> 64.3 us (0.970)
  Pallas kernels: 65.5 us -> 63.5 us
    pallas_call x1, Pallas kernels: 63.9 us -> 62 us  [fused(): pl.pallas_call(functools.partial(fused_kernel, cols, depth, group), out_s...]
where the time goes in v3:
time: 64.3 us; the launch traced here: 64.1 us
  Pallas kernels  63.5 us (99%)
    pallas_call x1, Pallas kernels, fused(): pl.pallas_call(functools.partial(fused_kernel, cols, depth, group), out_s...  62 us
    pallas_call x1, Pallas kernels, store(): pl.pallas_call(store_kernel, out_shape=tuple((jax.ShapeDtypeStruct(a.shap...  1.53 us

profile of v3, /device:TPU:0, one launch (start us, length us, event | category | flops | bytes accessed | tf_op | source)
XLA Modules:
  0.0 64.1 jit_solution(10057844745521764071)
XLA Ops:
  0.6 62.0 %shard_map.93 = (bf16[128,1024]{1,0:T(8,128)(2,1)S(1)}, bf16[8,128]{1,0:T(8,128)(2,1)S(1)}, bf16[1,1024,768]{2,1,0:T(8,128)(2,1)S(1)}, bf16[1,384,1024]{2,1,0:T(8,128)(2,1)S(1)}) custom-call(bf16[128,1024]{1,0:T(8,128)(2,1)} %tok_hbm.1, bf16[128,1024]{1,0:T(8,128)(2,1)} %up_hbm.1, s32[8,128]{1,0:T(8,128)} %bitcast.3, bf16[8,128]{1,0:T(8,128)(2,1)} %bitcast.4, ...), custom_call_target="tpu_custom_call" | custom-call | tf_op jit(solution)/shard_map/pallas_call | solution.py:632
  62.6 1.5 %shard_map.94 = (bf16[128,1024]{1,0:T(8,128)(2,1)}, bf16[8,128]{1,0:T(8,128)(2,1)}, bf16[1,1024,768]{2,1,0:T(8,128)(2,1)}, bf16[1,384,1024]{2,1,0:T(8,128)(2,1)}) custom-call(bf16[128,1024]{1,0:T(8,128)(2,1)S(1)} %get-tuple-element.12.refs_0_, bf16[8,128]{1,0:T(8,128)(2,1)S(1)} %get-tuple-element.13.refs_1_, ...), custom_call_target="tpu_custom_call" | custom-call | tf_op jit(solution)/shard_map/pallas_call | solution.py:574

commit v4 on v3

--- a/solution.py
+++ b/solution.py
@@ -10,6 +10,7 @@
 
 CORES = 2
 HALVES = 2
+SPLIT = 2
 MESH = pl.DeviceIdType.MESH
 
 
@@ -153,8 +154,9 @@
     cols, depth, group,
     tok_hbm, up_hbm, routes_hbm, gates_hbm, win_hbm, wout_hbm,
     tg_ref, gg_ref, gin_ref, gdown_ref,
-    routes_ref, gates_ref, tok, up, table, win, wout, xs, su, hid, gp, igs, igb, acc, cs, cr, rk, rx, scs, scr,
+    routes_ref, gates_ref, tok, up, table, win, wout, win_t, wout_t, xs, su, hid, gp, igs, igb, acc, cs, cr, rk, rx, scs, scr,
     load_sem, recv_sem, chart_sem, near_sem, near_chart_sem, igr_sem, cr_sem, rx_sem, scr_sem, sent_sem,
+    tail_sem, near_tail_sem, igr_tail_sem,
 ):
     da = lax.axis_index("da")
     z = lax.axis_index("db")
@@ -166,6 +168,8 @@
     rows = half // group
     ff = wout.shape[0]
     steps = HALVES * depth
+    part = half // SPLIT
+    few = rows // SPLIT
 
     def slot(xx, zz, cc):
         return (xx * CORES + cc) * depth + zz
@@ -274,9 +278,37 @@
         one(depth - 1 - z, 1)
         one(z, -1)
 
+    def last_part(xx, u, a, way, to_x, to_c, near=None):
+        ref = held[a].at[slot(xx, z, c), HALVES - 1, pl.ds(u * part, part)]
+        landed = near
+        if near is None:
+            landed = recv_sem.at[xx, z, HALVES - 1, a] if u == 0 else tail_sem.at[a]
+        return send(ref, ref, sent_sem.at[way], landed, to_x, z, to_c)
+
+    def last_from_across(u):
+        near = near_sem.at[steps - 1] if u == 0 else near_tail_sem.at[0]
+        for a in range(2):
+            last_part(1 - x, u, a, 1, 1 - x, c).wait_recv()
+            last_part(1 - x, u, a, 2, x, 1 - c, near).start()
+
+    def last_from_partner(u):
+        if u == 0:
+            settle(xs.at[pl.ds(0, (cols + 1) * half)], near_sem.at[steps - 1])
+        else:
+            settle(tok.at[0, 0], near_tail_sem.at[0])
+
     def across(i, a):
         zz, h = step_of(i)
-        both(x, zz, h, a, 1, start, 1 - x, z, c)
+
+        @pl.when(i < steps - 1)
+        def _():
+            both(x, zz, h, a, 1, start, 1 - x, z, c)
+
+        @pl.when(i == steps - 1)
+        def _():
+            for b in range(2):
+                last_part(x, a, b, 1, 1 - x, c).start()
+
         both(x, zz, h, a, 2, start, x, z, 1 - c, near=i)
 
     def from_across(i, a):
@@ -306,6 +338,12 @@
     def send_ig(q, k):
         return send(igs.at[k, q], igb.at[k, q, c], sent_sem.at[5], igr_sem.at[k, q], x, z, 1 - c)
 
+    def send_last_ig(q, u):
+        at = pl.ds(u * few, few)
+        landed = igr_sem.at[steps - 1, q] if u == 0 else igr_tail_sem.at[q]
+        src, dst = igs.at[steps - 1, q, at], igb.at[steps - 1, q, c, at]
+        return send(src, dst, sent_sem.at[5], landed, x, z, 1 - c)
+
     def send_score(s):
         return pltpu.make_async_remote_copy(
             src_ref=scs.at[s],
@@ -319,25 +357,34 @@
     blocks = [(q, r) for q in range(cols) for r in range(CORES)]
     batch = len(blocks) * rows
 
-    def compute(k):
-        zz, h = step_of(k)
-        base = pl.multiple_of(k * batch, batch)
+    def compute(k, u=None):
+        zz, h = step_of(k) if u is None else (z, HALVES - 1)
+        count_rows = rows if u is None else few
+        size = len(blocks) * count_rows
+        base = pl.multiple_of(k * batch, batch) if u is None else k * batch + u * size
         picks = []
         gate_cols = []
         for n, (q, r) in enumerate(blocks):
             s = slot((x + q) % cols, zz, (c + r) % CORES)
             chosen, row = pick(s, me, h)
+            tokens, upstreams = tok.at[s, h], up.at[s, h]
+            if u is not None:
+                span = slice(u * part, (u + 1) * part)
+                chosen, row = chosen[u * few : (u + 1) * few, span], row[:, span]
+                tokens = tokens.at[pl.ds(u * part, part)]
+                upstreams = upstreams.at[pl.ds(u * part, part)]
             picks.append((s, chosen))
             gate_cols.append(jnp.sum(chosen * row, axis=1, keepdims=True))
             hot = chosen.astype(jnp.bfloat16)
-            where = pl.ds(pl.multiple_of(base + n * rows, rows), rows)
-            xs[where, :] = dot(hot, tok[s, h], ((1,), (0,))).astype(jnp.bfloat16)
-            su[where, :] = dot(hot, up[s, h], ((1,), (0,))).astype(jnp.bfloat16)
-        here = pl.ds(base, batch)
+            where = base + n * count_rows
+            where = pl.ds(pl.multiple_of(where, count_rows) if u is None else where, count_rows)
+            xs[where, :] = dot(hot, tokens[...], ((1,), (0,))).astype(jnp.bfloat16)
+            su[where, :] = dot(hot, upstreams[...], ((1,), (0,))).astype(jnp.bfloat16)
+        here = pl.ds(base, size)
         gate = jnp.concatenate(gate_cols, axis=0)
         upstream = su[here, :]
         projected = dot(xs[here, :], win[...], ((1,), (0,)))
-        back_raw = dot(upstream, wout[...], ((1,), (1,)))
+        back_raw = dot(upstream, wout_t[...], ((1,), (0,)))
         su[here, :] = (gate * upstream.astype(jnp.float32)).astype(jnp.bfloat16)
         gate_part, up_part = projected[:, :ff], projected[:, ff:]
         activated, derivative = silu_parts(gate_part)
@@ -348,17 +395,37 @@
         back_hidden = gate * back_raw
         gp[here, :ff] = (back_hidden * up_part * derivative).astype(jnp.bfloat16)
         gp[here, ff:] = (back_hidden * activated).astype(jnp.bfloat16)
-        grads = dot(gp[here, :], win[...], ((1,), (1,))).astype(jnp.bfloat16)
+        grads = dot(gp[here, :], win_t[...], ((1,), (0,))).astype(jnp.bfloat16)
         for n, (q, r) in enumerate(blocks):
-            piece = grads[n * rows : (n + 1) * rows]
-            if r == 0:
-                igb[k, q, c] = piece
+            piece = grads[n * count_rows : (n + 1) * count_rows]
+            if u is None:
+                if r == 0:
+                    igb[k, q, c] = piece
+                else:
+                    igs[k, q] = piece
+                    send_ig(q, k).start()
             else:
-                igs[k, q] = piece
-                send_ig(q, k).start()
+                at = pl.ds(u * few, few)
+                if r == 0:
+                    igb[k, q, c, at] = piece
+                else:
+                    igs[k, q, at] = piece
+                    send_last_ig(q, u).start()
         for n, (q, r) in enumerate(blocks):
             s, chosen = picks[n]
-            line = jnp.sum(chosen * scores[n * rows : (n + 1) * rows], axis=0, keepdims=True)
+            line = jnp.sum(chosen * scores[n * count_rows : (n + 1) * count_rows], axis=0, keepdims=True)
+            if u is not None:
+                ahead = (HALVES - 1) * half + u * part
+                parts = [jnp.zeros((1, ahead), jnp.float32), line]
+                if u < SPLIT - 1:
+                    parts.append(jnp.zeros((1, local - ahead - part), jnp.float32))
+                scs[s] = scs[s] + jnp.broadcast_to(jnp.concatenate(parts, axis=1), scs.shape[1:])
+                if u == SPLIT - 1:
+                    if q == 0 and r == 0:
+                        scr[me] = scs[me]
+                    else:
+                        send_score(s).start()
+                continue
             rest = jnp.zeros_like(line)
             first = jnp.concatenate([line, rest], axis=1)
             second = jnp.concatenate([rest, line], axis=1)
@@ -370,68 +437,89 @@
             @pl.when(h == 1)
             def _():
                 scs[s] = scs[s] + jnp.broadcast_to(second, scs.shape[1:])
-                if q == 0 and r == 0:
-
-                    @pl.when(zz == z)
-                    def _():
-                        scr[me] = scs[me]
-
-                    @pl.when(zz != z)
-                    def _():
-                        send_score(s).start()
-                else:
-                    send_score(s).start()
-
-    def chip_sum(k, q):
-        zz, h = step_of(k)
-        s = slot((x + q) % cols, zz, c)
-        hot = jnp.concatenate([pick(s, slot(x, z, m), h)[0] for m in range(CORES)], axis=0)
-        pair = igb[k, q].reshape(CORES * rows, features)
-        return dot(hot.astype(jnp.bfloat16), pair, ((0,), (0,)))
-
-    def send_sum(zz, h, q, side, to_z):
+                send_score(s).start()
+
+    def send_sum(zz, h, q, u, side, to_z):
         place = jnp.where((zz == to_z) & (side == 1), depth, zz)
-        landed = cr.at[place, h, q]
-        return send(cs.at[zz, h, q], landed, sent_sem.at[6], cr_sem.at[place, h, q], x, to_z, c)
-
-    def send_across(h):
-        return send(cs.at[z, h, 1], rx.at[h], sent_sem.at[6], rx_sem.at[h], 1 - x, z, c)
+        at = pl.ds(u * part, part) if q else pl.ds(0, half)
+        landed = cr_sem.at[place, h, q + u]
+        return send(cs.at[zz, h, q, at], cr.at[place, h, q, at], sent_sem.at[6], landed, x, to_z, c)
+
+    def send_across(h, u=None):
+        at = pl.ds(0, half) if u is None else pl.ds(u * part, part)
+        landed = rx_sem.at[0 if u is None else 1 + u]
+        return send(cs.at[z, h, 1, at], rx.at[h, at], sent_sem.at[6], landed, 1 - x, z, c)
+
+    def gather(zz, h, q, u, total):
+        at = pl.ds(u * part, part) if q else pl.ds(0, half)
+        to = pl.ds(0, part if q else half)
+        acc[to, :] = total
+        for side, ok in ((0, (zz <= z) & (z < depth - 1)), (1, (zz >= z) & (z > 0))):
+
+            @pl.when(ok)
+            def _():
+                send_sum(zz, h, q, u, side, z).wait_recv()
+                place = jnp.where((zz == z) & (side == 1), depth, zz)
+                acc[to, :] += cr[place, h, q, at].astype(jnp.float32)
+
+        return at, to
+
+    def hot_of(s, h):
+        return [pick(s, slot(x, z, m), h)[0] for m in range(CORES)]
 
     def pass_on(k, q):
         zz, h = step_of(k)
+        hot = jnp.concatenate(hot_of(slot((x + q) % cols, zz, c), h), axis=0).astype(jnp.bfloat16)
         send_ig(q, k).wait_recv()
-        acc[...] = chip_sum(k, q)
-        for side, ok in ((0, (zz <= z) & (z < depth - 1)), (1, (zz >= z) & (z > 0))):
-
-            @pl.when(ok)
+        pair = igb[k, q].reshape(CORES * rows, features)
+        for u in range(SPLIT if q else 1):
+            mine = hot[:, u * part : (u + 1) * part] if q else hot
+            at, to = gather(zz, h, q, u, dot(mine, pair, ((0,), (0,))))
+            cs[zz, h, q, at] = acc[to, :].astype(jnp.bfloat16)
+
+            @pl.when(zz < z)
             def _():
-                send_sum(zz, h, q, side, z).wait_recv()
-                place = jnp.where((zz == z) & (side == 1), depth, zz)
-                acc[...] += cr[place, h, q].astype(jnp.float32)
-
-        if q == 0:
-
-            @pl.when(zz == z)
+                send_sum(zz, h, q, u, 0, z - 1).start()
+
+            @pl.when(zz > z)
             def _():
-                rk[h] = acc[...]
-
-        @pl.when((zz != z) if q == 0 else True)
-        def _():
-            cs[zz, h, q] = acc[...].astype(jnp.bfloat16)
-
-        @pl.when(zz < z)
-        def _():
-            send_sum(zz, h, q, 0, z - 1).start()
-
-        @pl.when(zz > z)
-        def _():
-            send_sum(zz, h, q, 1, z + 1).start()
-
-        if q == 1:
-
-            @pl.when(zz == z)
-            def _():
-                send_across(h).start()
+                send_sum(zz, h, q, u, 1, z + 1).start()
+
+    def home_sum(k, h, q):
+        hot = jnp.concatenate(hot_of(slot((x + q) % cols, z, c), h), axis=0).astype(jnp.bfloat16)
+        pair = igb[k, q].reshape(CORES * rows, features)
+        return hot, pair
+
+    def home_first():
+        send_ig(1, 0).wait_recv()
+        hot, pair = home_sum(0, 0, 1)
+        for u in range(SPLIT):
+            span = slice(u * part, (u + 1) * part)
+            at, to = gather(z, 0, 1, u, dot(hot[:, span], pair, ((0,), (0,))))
+            cs[z, 0, 1, at] = acc[to, :].astype(jnp.bfloat16)
+        send_across(0).start()
+
+    def home_last(u):
+        k = steps - 1
+        s = slot(1 - x, z, c)
+        here, span = slice(u * few, (u + 1) * few), slice(u * part, (u + 1) * part)
+        hot = jnp.concatenate([one[here, span] for one in hot_of(s, HALVES - 1)], axis=0)
+        send_last_ig(1, u).wait_recv()
+        pair = igb[k, 1, :, pl.ds(u * few, few)].reshape(CORES * few, features)
+        at, to = gather(z, HALVES - 1, 1, u, dot(hot.astype(jnp.bfloat16), pair, ((0,), (0,))))
+        cs[z, HALVES - 1, 1, at] = acc[to, :].astype(jnp.bfloat16)
+        send_across(HALVES - 1, u).start()
+
+    def home_own():
+        for k, h in ((0, 0), (steps - 1, HALVES - 1)):
+            if h == 0:
+                send_ig(0, 0).wait_recv()
+            else:
+                for u in range(SPLIT):
+                    send_last_ig(0, u).wait_recv()
+            hot, pair = home_sum(k, h, 0)
+            gather(z, h, 0, 0, dot(hot, pair, ((0,), (0,))))
+            rk[h] = acc[...]
 
     words = lag_words(depth)
     word = jnp.int32(words[0])
@@ -467,6 +555,8 @@
         def _():
             loads[4].wait()
             loads[5].wait()
+            win_t[...] = win[...].T
+            wout_t[...] = wout[...].T
 
         @pl.when(inner & (i >= 2))
         def _():
@@ -476,13 +566,9 @@
         def _():
             from_across(i - 1, 1)
 
-        @pl.when(inner & (i >= 2) & (i < steps))
+        @pl.when(inner & (i >= 2))
         def _():
             pass_all(i, 0)
-
-        @pl.when(i == steps)
-        def _():
-            pass_on(0, 1)
 
         @pl.when(i >= 1)
         def _():
@@ -494,30 +580,51 @@
             along_z(i + 1, 0)
             across(i + 1, 0)
 
-        @pl.when(i < steps)
+        @pl.when(i < steps - 1)
         def _():
             from_across(i, 0)
 
-        @pl.when(edge & (i >= 1) & (i < steps))
+        @pl.when(i == steps - 1)
+        def _():
+            last_from_across(0)
+
+        @pl.when(edge & (i >= 1))
         def _():
             pass_all(i + 1, 1)
             pass_all(i + 1, 0)
 
         return carry
 
-    lax.fori_loop(0, steps + 1, step, 0)
+    lax.fori_loop(0, steps, step, 0)
+
+    @pl.when(inner)
+    def _():
+        pass_all(steps, 1)
+
+    last_from_partner(0)
+    compute(steps - 1, 0)
+    last_from_across(1)
+    home_first()
+
     @pl.when(inner)
     def _():
         pass_all(steps, 0)
 
-    pass_on(steps - 1, 1)
+    last_from_partner(1)
+    compute(steps - 1, 1)
+    home_last(0)
 
     wide = min(features, 256)
 
-    @pl.loop(0, features // wide)
-    def _(t):
+    def gin(t, carry):
         at = pl.ds(pl.multiple_of(t * wide, wide), wide)
         gin_ref[0, at, :] = dot(xs[:, at], gp[...], ((0,), (0,))).astype(jnp.bfloat16)
+        return carry
+
+    early = jnp.where(edge, 1, 1)
+    lax.fori_loop(0, early, gin, 0)
+    home_last(1)
+    lax.fori_loop(early, features // wide, gin, 0)
 
     thin = 128
 
@@ -526,8 +633,7 @@
         at = pl.ds(pl.multiple_of(t * thin, thin), thin)
         gdown_ref[0, at, :] = dot(hid[:, at], su[...], ((0,), (0,))).astype(jnp.bfloat16)
 
-    pass_on(0, 0)
-    pass_on(steps - 1, 0)
+    home_own()
     settle(scr.at[pl.ds(0, count - 1)], scr_sem.at[0])
     scores = scr[:, 0, :]
     place = lax.broadcasted_iota(jnp.int32, (top, local), 0)
@@ -538,7 +644,8 @@
     gg_ref[...] = gate_grads.astype(jnp.bfloat16)
 
     for h in range(HALVES):
-        send_across(h).wait_recv()
+        for u in (None,) if h == 0 else range(SPLIT):
+            send_across(h, u).wait_recv()
         tg_ref[pl.ds(h * half, half), :] = (rk[h] + rx[h].astype(jnp.float32)).astype(jnp.bfloat16)
 
     for at in range(depth):
@@ -603,6 +710,8 @@
         pltpu.VMEM((experts, experts, local), bf),
         pltpu.VMEM((features, 2 * ff), bf),
         pltpu.VMEM((ff, features), bf),
+        pltpu.VMEM((2 * ff, features), bf),
+        pltpu.VMEM((features, ff), bf),
         pltpu.VMEM((total, features), bf),
         pltpu.VMEM((total, features), bf),
         pltpu.VMEM((total, ff), bf),
@@ -622,10 +731,13 @@
         dma((steps,)),
         dma((depth,)),
         dma((steps, cols)),
-        dma((depth + 1, HALVES, cols)),
-        dma((HALVES,)),
+        dma((depth + 1, HALVES, 1 + SPLIT)),
+        dma((1 + SPLIT,)),
         dma((1,)),
         dma((8,)),
+        dma((2,)),
+        dma((1,)),
+        dma((cols,)),
     ]
     vmem = pl.BlockSpec(memory_space=pltpu.VMEM)
     hbm = pl.BlockSpec(memory_space=pltpu.HBM)
@@ -668,7 +780,7 @@
         and local == 128
         and experts <= local
         and max(map(max, relay_slots(lax.axis_size("db")))) == HALVES * lax.axis_size("db") + 1
-        and (local // (HALVES * group)) % 16 == 0
+        and (local // (HALVES * SPLIT * group)) % 16 == 0
         and w_down.shape[1] % 128 == 0
     )
 

time: 64.3 us -> 63.1 us (0.981)
  Pallas kernels: 63.5 us -> 62.3 us
    pallas_call x1, Pallas kernels: 62 us -> 60.8 us  [fused(): pl.pallas_call(functools.partial(fused_kernel, cols, depth, group), out_s...]
where the time goes in v4:
time: 63.1 us; the launch traced here: 62.9 us
  Pallas kernels  62.3 us (99%)
  between operations  0.64 us (1%)
    pallas_call x1, Pallas kernels, fused(): pl.pallas_call(functools.partial(fused_kernel, cols, depth, group), out_s...  60.8 us
    pallas_call x1, Pallas kernels, store(): pl.pallas_call(store_kernel, out_shape=tuple((jax.ShapeDtypeStruct(a.shap...  1.53 us

profile of v4, /device:TPU:0, one launch (start us, length us, event | category | flops | bytes accessed | tf_op | source)
XLA Modules:
  0.0 62.9 jit_solution(7072019275988440968)
XLA Ops:
  0.6 60.8 %shard_map.93 = (bf16[128,1024]{1,0:T(8,128)(2,1)S(1)}, bf16[8,128]{1,0:T(8,128)(2,1)S(1)}, bf16[1,1024,768]{2,1,0:T(8,128)(2,1)S(1)}, bf16[1,384,1024]{2,1,0:T(8,128)(2,1)S(1)}) custom-call(bf16[128,1024]{1,0:T(8,128)(2,1)} %tok_hbm.1, bf16[128,1024]{1,0:T(8,128)(2,1)} %up_hbm.1, s32[8,128]{1,0:T(8,128)} %bitcast.3, bf16[8,128]{1,0:T(8,128)(2,1)} %bitcast.4, ...), custom_call_target="tpu_custom_call" | custom-call | tf_op jit(solution)/shard_map/pallas_call | solution.py:744
  61.4 1.5 %shard_map.94 = (bf16[128,1024]{1,0:T(8,128)(2,1)}, bf16[8,128]{1,0:T(8,128)(2,1)}, bf16[1,1024,768]{2,1,0:T(8,128)(2,1)}, bf16[1,384,1024]{2,1,0:T(8,128)(2,1)}) custom-call(bf16[128,1024]{1,0:T(8,128)(2,1)S(1)} %get-tuple-element.12.refs_0_, bf16[8,128]{1,0:T(8,128)(2,1)S(1)} %get-tuple-element.13.refs_1_, ...), custom_call_target="tpu_custom_call" | custom-call | tf_op jit(solution)/shard_map/pallas_call | solution.py:681

commit v5 on v4

--- a/solution.py
+++ b/solution.py
@@ -154,8 +154,8 @@
     cols, depth, group,
     tok_hbm, up_hbm, routes_hbm, gates_hbm, win_hbm, wout_hbm,
     tg_ref, gg_ref, gin_ref, gdown_ref,
-    routes_ref, gates_ref, tok, up, table, win, wout, win_t, wout_t, xs, su, hid, gp, igs, igb, acc, cs, cr, rk, rx, scs, scr,
-    load_sem, recv_sem, chart_sem, near_sem, near_chart_sem, igr_sem, cr_sem, rx_sem, scr_sem, sent_sem,
+    routes_ref, gates_ref, tok, up, table, win, wout, win_t, wout_t, xs, su, hid, gp, igs, igb, acc, cs, cr, rk, rx, scs, scr, bulk,
+    load_sem, recv_sem, near_sem, igr_sem, cr_sem, rx_sem, scr_sem, sent_sem,
     tail_sem, near_tail_sem, igr_tail_sem,
 ):
     da = lax.axis_index("da")
@@ -245,14 +245,23 @@
         s = slot(xx, zz, c)
         ref = held[a].at[s, h]
         landed = recv_sem.at[xx, zz, h, a] if near is None else near_sem.at[near]
-        act(send(ref, ref, sent_sem.at[way], landed, to_x, to_z, to_c))
-        if a == 0:
-
-            @pl.when(h == 0)
-            def _():
-                ref = table.at[s]
-                landed = chart_sem.at[xx, zz] if near is None else near_chart_sem.at[zz]
-                act(send(ref, ref, sent_sem.at[3 + (way > 0)], landed, to_x, to_z, to_c))
+        copy = send(ref, ref, sent_sem.at[way], landed, to_x, to_z, to_c)
+        if a != 0:
+            act(copy)
+            return
+
+        @pl.when(h != 0)
+        def _():
+            act(copy)
+
+        @pl.when(h == 0)
+        def _():
+            if act is start:
+                copy.start()
+                page = table.at[s]
+                send(page, page, sent_sem.at[3 + (way > 0)], landed, to_x, to_z, to_c).start()
+            else:
+                settle(bulk.at[pl.ds(0, half * features // 128 + experts)], landed)
 
     def step_of(i):
         j = jnp.minimum(i, steps - 1 - i)
@@ -318,11 +327,14 @@
 
     def from_partner(i):
         zz, h = step_of(i)
-        settle(tok.at[pl.ds(0, cols)], near_sem.at[i])
 
         @pl.when(h == 0)
         def _():
-            settle(table.at[pl.ds(0, cols)], near_chart_sem.at[zz])
+            settle(bulk, near_sem.at[i])
+
+        @pl.when(h != 0)
+        def _():
+            settle(tok.at[pl.ds(0, cols)], near_sem.at[i])
 
     def pick(s, e, h):
         chart_s = table[s].astype(jnp.float32)
@@ -336,11 +348,11 @@
         return jnp.where(hit, 1.0, 0.0), row
 
     def send_ig(q, k):
-        return send(igs.at[k, q], igb.at[k, q, c], sent_sem.at[5], igr_sem.at[k, q], x, z, 1 - c)
+        return send(igs.at[k, q], igb.at[k, q, c], sent_sem.at[5], igr_sem.at[k], x, z, 1 - c)
 
     def send_last_ig(q, u):
         at = pl.ds(u * few, few)
-        landed = igr_sem.at[steps - 1, q] if u == 0 else igr_tail_sem.at[q]
+        landed = igr_sem.at[steps - 1] if u == 0 else igr_tail_sem.at[0]
         src, dst = igs.at[steps - 1, q, at], igb.at[steps - 1, q, c, at]
         return send(src, dst, sent_sem.at[5], landed, x, z, 1 - c)
 
@@ -470,7 +482,8 @@
     def pass_on(k, q):
         zz, h = step_of(k)
         hot = jnp.concatenate(hot_of(slot((x + q) % cols, zz, c), h), axis=0).astype(jnp.bfloat16)
-        send_ig(q, k).wait_recv()
+        if q == 1:
+            settle(igs.at[0], igr_sem.at[k])
         pair = igb[k, q].reshape(CORES * rows, features)
         for u in range(SPLIT if q else 1):
             mine = hot[:, u * part : (u + 1) * part] if q else hot
@@ -491,7 +504,7 @@
         return hot, pair
 
     def home_first():
-        send_ig(1, 0).wait_recv()
+        settle(igs.at[0], igr_sem.at[0])
         hot, pair = home_sum(0, 0, 1)
         for u in range(SPLIT):
             span = slice(u * part, (u + 1) * part)
@@ -504,7 +517,7 @@
         s = slot(1 - x, z, c)
         here, span = slice(u * few, (u + 1) * few), slice(u * part, (u + 1) * part)
         hot = jnp.concatenate([one[here, span] for one in hot_of(s, HALVES - 1)], axis=0)
-        send_last_ig(1, u).wait_recv()
+        settle(igs.at[0, 0], igr_sem.at[k] if u == 0 else igr_tail_sem.at[0])
         pair = igb[k, 1, :, pl.ds(u * few, few)].reshape(CORES * few, features)
         at, to = gather(z, HALVES - 1, 1, u, dot(hot.astype(jnp.bfloat16), pair, ((0,), (0,))))
         cs[z, HALVES - 1, 1, at] = acc[to, :].astype(jnp.bfloat16)
@@ -512,11 +525,6 @@
 
     def home_own():
         for k, h in ((0, 0), (steps - 1, HALVES - 1)):
-            if h == 0:
-                send_ig(0, 0).wait_recv()
-            else:
-                for u in range(SPLIT):
-                    send_last_ig(0, u).wait_recv()
             hot, pair = home_sum(k, h, 0)
             gather(z, h, 0, 0, dot(hot, pair, ((0,), (0,))))
             rk[h] = acc[...]
@@ -621,7 +629,7 @@
         gin_ref[0, at, :] = dot(xs[:, at], gp[...], ((0,), (0,))).astype(jnp.bfloat16)
         return carry
 
-    early = jnp.where(edge, 1, 1)
+    early = jnp.where(edge, 2, 1)
     lax.fori_loop(0, early, gin, 0)
     home_last(1)
     lax.fori_loop(early, features // wide, gin, 0)
@@ -725,19 +733,18 @@
         pltpu.VMEM((HALVES, half, features), bf),
         pltpu.VMEM((experts, 8, local), f32),
         pltpu.VMEM((experts, 8, local), f32),
+        pltpu.VMEM((2 * cols * half * features // 128 + cols * experts, 128), bf),
         dma((5,)),
         dma((cols, depth, HALVES, 2)),
-        dma((cols, depth)),
         dma((steps,)),
-        dma((depth,)),
-        dma((steps, cols)),
+        dma((steps,)),
         dma((depth + 1, HALVES, 1 + SPLIT)),
         dma((1 + SPLIT,)),
         dma((1,)),
         dma((8,)),
         dma((2,)),
         dma((1,)),
-        dma((cols,)),
+        dma((1,)),
     ]
     vmem = pl.BlockSpec(memory_space=pltpu.VMEM)
     hbm = pl.BlockSpec(memory_space=pltpu.HBM)

time: 63.1 us -> 62.8 us (level)
  no operation moved by 1% of the time
where the time goes in v5:
time: 62.8 us; the launch traced here: 62.6 us
  Pallas kernels  62 us (99%)
  between operations  0.64 us (1%)
    pallas_call x1, Pallas kernels, fused(): pl.pallas_call(functools.partial(fused_kernel, cols, depth, group), out_s...  60.5 us
    pallas_call x1, Pallas kernels, store(): pl.pallas_call(store_kernel, out_shape=tuple((jax.ShapeDtypeStruct(a.shap...  1.53 us

profile of v5, /device:TPU:0, one launch (start us, length us, event | category | flops | bytes accessed | tf_op | source)
XLA Modules:
  0.0 62.6 jit_solution(8572350338936644694)
XLA Ops:
  0.6 60.5 %shard_map.93 = (bf16[128,1024]{1,0:T(8,128)(2,1)S(1)}, bf16[8,128]{1,0:T(8,128)(2,1)S(1)}, bf16[1,1024,768]{2,1,0:T(8,128)(2,1)S(1)}, bf16[1,384,1024]{2,1,0:T(8,128)(2,1)S(1)}) custom-call(bf16[128,1024]{1,0:T(8,128)(2,1)} %tok_hbm.1, bf16[128,1024]{1,0:T(8,128)(2,1)} %up_hbm.1, s32[8,128]{1,0:T(8,128)} %bitcast.3, bf16[8,128]{1,0:T(8,128)(2,1)} %bitcast.4, ...), custom_call_target="tpu_custom_call" | custom-call | tf_op jit(solution)/shard_map/pallas_call | solution.py:751
  61.1 1.5 %shard_map.94 = (bf16[128,1024]{1,0:T(8,128)(2,1)}, bf16[8,128]{1,0:T(8,128)(2,1)}, bf16[1,1024,768]{2,1,0:T(8,128)(2,1)}, bf16[1,384,1024]{2,1,0:T(8,128)(2,1)}) custom-call(bf16[128,1024]{1,0:T(8,128)(2,1)S(1)} %get-tuple-element.12.refs_0_, bf16[8,128]{1,0:T(8,128)(2,1)S(1)} %get-tuple-element.13.refs_1_, ...), custom_call_target="tpu_custom_call" | custom-call | tf_op jit(solution)/shard_map/pallas_call | solution.py:689

commit v6 on v5

--- a/solution.py
+++ b/solution.py
@@ -651,25 +651,25 @@
         gate_grads = jnp.where(place == k, value, gate_grads)
     gg_ref[...] = gate_grads.astype(jnp.bfloat16)
 
+    for at in range(depth):
+        sent = (depth - at if at > 0 else 0) + (at + 1 if at < depth - 1 else 0)
+
+        @pl.when(z == at)
+        def _():
+            settle(tok.at[pl.ds(0, 2 * sent)], sent_sem.at[0])
+            settle(table.at[pl.ds(0, sent)], sent_sem.at[3])
+
+    settle(tok.at[pl.ds(0, 2 * depth)], sent_sem.at[1])
+    settle(tok, sent_sem.at[2])
+    settle(table.at[pl.ds(0, 3 * depth)], sent_sem.at[4])
+    settle(igs, sent_sem.at[5])
+    settle(scs.at[pl.ds(0, count - 1)], sent_sem.at[7])
+
     for h in range(HALVES):
         for u in (None,) if h == 0 else range(SPLIT):
             send_across(h, u).wait_recv()
         tg_ref[pl.ds(h * half, half), :] = (rk[h] + rx[h].astype(jnp.float32)).astype(jnp.bfloat16)
-
-    for at in range(depth):
-        sent = (depth - at if at > 0 else 0) + (at + 1 if at < depth - 1 else 0)
-
-        @pl.when(z == at)
-        def _():
-            settle(tok.at[pl.ds(0, 2 * sent)], sent_sem.at[0])
-            settle(table.at[pl.ds(0, sent)], sent_sem.at[3])
-
-    settle(tok.at[pl.ds(0, 2 * depth)], sent_sem.at[1])
-    settle(tok, sent_sem.at[2])
-    settle(table.at[pl.ds(0, 3 * depth)], sent_sem.at[4])
-    settle(igs, sent_sem.at[5])
     settle(tok.at[pl.ds(0, depth * cols - 1)], sent_sem.at[6])
-    settle(scs.at[pl.ds(0, count - 1)], sent_sem.at[7])
 
 
 def store_kernel(*refs):

time: 62.8 us -> 62.8 us (level)
  no operation moved by 1% of the time
where the time goes in v6:
time: 62.8 us; the launch traced here: 62.6 us
  Pallas kernels  62 us (99%)
  between operations  0.64 us (1%)
    pallas_call x1, Pallas kernels, fused(): pl.pallas_call(functools.partial(fused_kernel, cols, depth, group), out_s...  60.4 us
    pallas_call x1, Pallas kernels, store(): pl.pallas_call(store_kernel, out_shape=tuple((jax.ShapeDtypeStruct(a.shap...  1.53 us

profile of v6, /device:TPU:0, one launch (start us, length us, event | category | flops | bytes accessed | tf_op | source)
XLA Modules:
  0.0 62.6 jit_solution(7100169601845395165)
XLA Ops:
  0.6 60.4 %shard_map.93 = (bf16[128,1024]{1,0:T(8,128)(2,1)S(1)}, bf16[8,128]{1,0:T(8,128)(2,1)S(1)}, bf16[1,1024,768]{2,1,0:T(8,128)(2,1)S(1)}, bf16[1,384,1024]{2,1,0:T(8,128)(2,1)S(1)}) custom-call(bf16[128,1024]{1,0:T(8,128)(2,1)} %tok_hbm.1, bf16[128,1024]{1,0:T(8,128)(2,1)} %up_hbm.1, s32[8,128]{1,0:T(8,128)} %bitcast.3, bf16[8,128]{1,0:T(8,128)(2,1)} %bitcast.4, ...), custom_call_target="tpu_custom_call" | custom-call | tf_op jit(solution)/shard_map/pallas_call | solution.py:751
  61.1 1.5 %shard_map.94 = (bf16[128,1024]{1,0:T(8,128)(2,1)}, bf16[8,128]{1,0:T(8,128)(2,1)}, bf16[1,1024,768]{2,1,0:T(8,128)(2,1)}, bf16[1,384,1024]{2,1,0:T(8,128)(2,1)}) custom-call(bf16[128,1024]{1,0:T(8,128)(2,1)S(1)} %get-tuple-element.12.refs_0_, bf16[8,128]{1,0:T(8,128)(2,1)S(1)} %get-tuple-element.13.refs_1_, ...), custom_call_target="tpu_custom_call" | custom-call | tf_op jit(solution)/shard_map/pallas_call | solution.py:689

commit v7 on v5

--- a/solution.py
+++ b/solution.py
@@ -651,10 +651,13 @@
         gate_grads = jnp.where(place == k, value, gate_grads)
     gg_ref[...] = gate_grads.astype(jnp.bfloat16)
 
-    for h in range(HALVES):
+    def finish(h):
         for u in (None,) if h == 0 else range(SPLIT):
             send_across(h, u).wait_recv()
         tg_ref[pl.ds(h * half, half), :] = (rk[h] + rx[h].astype(jnp.float32)).astype(jnp.bfloat16)
+
+    for h in range(HALVES - 1):
+        finish(h)
 
     for at in range(depth):
         sent = (depth - at if at > 0 else 0) + (at + 1 if at < depth - 1 else 0)
@@ -668,8 +671,10 @@
     settle(tok, sent_sem.at[2])
     settle(table.at[pl.ds(0, 3 * depth)], sent_sem.at[4])
     settle(igs, sent_sem.at[5])
+    settle(scs.at[pl.ds(0, count - 1)], sent_sem.at[7])
+
+    finish(HALVES - 1)
     settle(tok.at[pl.ds(0, depth * cols - 1)], sent_sem.at[6])
-    settle(scs.at[pl.ds(0, count - 1)], sent_sem.at[7])
 
 
 def store_kernel(*refs):

time: 62.8 us -> 62.8 us (level)
  no operation moved by 1% of the time
where the time goes in v7:
time: 62.8 us; the launch traced here: 62.6 us
  Pallas kernels  62 us (99%)
  between operations  0.64 us (1%)
    pallas_call x1, Pallas kernels, fused(): pl.pallas_call(functools.partial(fused_kernel, cols, depth, group), out_s...  60.4 us
    pallas_call x1, Pallas kernels, store(): pl.pallas_call(store_kernel, out_shape=tuple((jax.ShapeDtypeStruct(a.shap...  1.53 us

profile of v7, /device:TPU:0, one launch (start us, length us, event | category | flops | bytes accessed | tf_op | source)
XLA Modules:
  0.0 62.6 jit_solution(10377791124253751512)
XLA Ops:
  0.6 60.4 %shard_map.93 = (bf16[128,1024]{1,0:T(8,128)(2,1)S(1)}, bf16[8,128]{1,0:T(8,128)(2,1)S(1)}, bf16[1,1024,768]{2,1,0:T(8,128)(2,1)S(1)}, bf16[1,384,1024]{2,1,0:T(8,128)(2,1)S(1)}) custom-call(bf16[128,1024]{1,0:T(8,128)(2,1)} %tok_hbm.1, bf16[128,1024]{1,0:T(8,128)(2,1)} %up_hbm.1, s32[8,128]{1,0:T(8,128)} %bitcast.3, bf16[8,128]{1,0:T(8,128)(2,1)} %bitcast.4, ...), custom_call_target="tpu_custom_call" | custom-call | tf_op jit(solution)/shard_map/pallas_call | solution.py:756
  61.1 1.5 %shard_map.94 = (bf16[128,1024]{1,0:T(8,128)(2,1)}, bf16[8,128]{1,0:T(8,128)(2,1)}, bf16[1,1024,768]{2,1,0:T(8,128)(2,1)}, bf16[1,384,1024]{2,1,0:T(8,128)(2,1)}) custom-call(bf16[128,1024]{1,0:T(8,128)(2,1)S(1)} %get-tuple-element.12.refs_0_, bf16[8,128]{1,0:T(8,128)(2,1)S(1)} %get-tuple-element.13.refs_1_, ...), custom_call_target="tpu_custom_call" | custom-call | tf_op jit(solution)/shard_map/pallas_call | solution.py:694
